TPU v7x, 256 devices: a whole 4x4x8 slice. The times are simulated.
256 devices in a mesh: row: 32 (over y_hi, z, core), col: 8 (over y_lo, x).
Axes of the slice: x: 4, y: 4 (y_hi: 2, y_lo: 2; y = y_hi * 2 + y_lo), z: 8, core: 2. Of those that a mesh axis runs over, the one named last changes fastest.
Arguments:
- velocity: float32 [6, 3, 16384], P(None, None, ('row', 'col')), may hold values from -3 to 3
- points: float32 [3, 16384], P(None, ('row', 'col')), may hold values from -1 to 1
- panel_area: float32 [16384], P(('row', 'col')), may hold values from 0.00048828125 to 0.0048828125
- self_term: float32 [16384], P(('row', 'col')), may hold values from 0.5 to 4
- near_index: int32 [16384, 128], P('row', 'col'), may hold values from 0 to 2047
- near_weight: float32 [16384, 128], P('row', 'col'), may hold values from -0.5 to 0.5
Outputs:
- density: float32 [6, 3, 16384], P(None, None, ('row', 'col'))
Inputs may be any that keep to these rules, and one draw needn't show every extreme that they name: `near_index`: each entry is a place in the source block of its column of 16 entries; places may repeat, and every listing counts.
All inputs are finite; a program needn't handle non-finite values.
Results may differ from a plain program's by a relative error of at most 0.0003.
Values sent between devices are 32-bit elements; how exact they have to be, the bound alone decides.
A program may use at most 128 MiB of HBM per device.

v0:
```python
import math

import jax
import jax.numpy as jnp
from jax import lax
from jax.sharding import PartitionSpec as P

ITERS = 3


BLOB_SQ = 0.0025
INV_EIGHT_PI = 1.0 / (8.0 * math.pi)


def build_columns(values, src_points):
    rhs_count = values.shape[0]
    count = values.shape[2]
    inner_prod = jnp.sum(src_points[None] * values, axis=1)
    direct_cols = values.reshape(rhs_count * 3, count)
    outer_cols = (src_points[None, :, None, :] * values[:, None, :, :]).reshape(
        rhs_count * 9, count
    )
    scaled = (src_points[None] * inner_prod[:, None]).reshape(rhs_count * 3, count)
    return (direct_cols, jnp.concatenate([direct_cols, inner_prod, outer_cols, scaled], axis=0))


def tile_terms(tgt_points, src_points, src_area, direct_cols, columns):
    offsets = tgt_points[:, :, None] - src_points[:, None, :]
    dist_sq = jnp.sum(offsets * offsets, axis=0)
    inv_root = lax.rsqrt(dist_sq + BLOB_SQ)
    kernel_two = src_area[None, :] * inv_root * inv_root * inv_root * INV_EIGHT_PI
    kernel_one = (dist_sq + 2.0 * BLOB_SQ) * kernel_two
    dims = (((1,), (1,)), ((), ()))
    near_one = lax.dot_general(direct_cols, kernel_one, dims, precision=lax.Precision.HIGHEST)
    products = lax.dot_general(columns, kernel_two, dims, precision=lax.Precision.HIGHEST)
    rhs_count = direct_cols.shape[0] // 3
    tgt_count = tgt_points.shape[1]
    direct = near_one.reshape(rhs_count, 3, tgt_count)
    along_f = products[: 3 * rhs_count].reshape(rhs_count, 3, tgt_count)
    along_g = products[3 * rhs_count : 4 * rhs_count]
    along_yf = products[4 * rhs_count : 13 * rhs_count].reshape(rhs_count, 3, 3, tgt_count)
    along_yg = products[13 * rhs_count :].reshape(rhs_count, 3, tgt_count)
    x_dot = jnp.sum(tgt_points[None] * along_f, axis=1)
    cross_term = jnp.sum(tgt_points[None, None] * along_yf, axis=2)
    return direct + tgt_points[None] * (x_dot - along_g)[:, None] - cross_term + along_yg


def solve_small(hessen, start_norm, count):
    zero = jnp.zeros_like(start_norm)
    target = [start_norm] + [zero] * count
    cosines = []
    sines = []
    triangle = {}
    for k in range(count):
        column = [hessen[i, k] for i in range(k + 2)]
        for j in range(k):
            first_val = column[j]
            second_val = column[j + 1]
            column[j] = cosines[j] * first_val + sines[j] * second_val
            column[j + 1] = cosines[j] * second_val - sines[j] * first_val
        radius = jnp.sqrt(column[k] * column[k] + column[k + 1] * column[k + 1])
        cosine = column[k] / radius
        sine = column[k + 1] / radius
        cosines.append(cosine)
        sines.append(sine)
        for i in range(k):
            triangle[i, k] = column[i]
        triangle[k, k] = radius
        target[k + 1] = -sine * target[k]
        target[k] = cosine * target[k]
    coeffs = [None] * count
    for k in range(count - 1, -1, -1):
        accum = target[k]
        for i in range(k + 1, count):
            accum = accum - triangle[k, i] * coeffs[i]
        coeffs[k] = accum / triangle[k, k]
    return coeffs


def block_size(length):
    best = 1
    for cand in range(1, min(length, 1024) + 1):
        if length % cand == 0:
            best = cand
    return best


def body(velocity, points, panel_area, self_term, near_index, near_weight):
    tgt_points = lax.all_gather(points, "col", axis=1, tiled=True)
    src_points, src_area = (
        lax.all_gather(points, "row", axis=1, tiled=True),
        lax.all_gather(panel_area, "row", axis=0, tiled=True),
    )
    rhs_count = velocity.shape[0]
    tgt_count = tgt_points.shape[1]
    empty = jnp.zeros((rhs_count, 3, tgt_count), jnp.float32)

    def norm_of(field):
        return jnp.sqrt(lax.psum(jnp.sum(field * field, axis=(1, 2)), ("row", "col")))

    start_norm = norm_of(velocity)
    basis = [velocity / start_norm[:, None, None]]
    hessen = {}
    for k in range(ITERS):
        vector = basis[k]
        gathered = lax.all_gather(vector, "row", axis=2, tiled=True)
        length = gathered.shape[2]
        step = block_size(length)
        turns = length // step
        direct_cols, columns = build_columns(gathered, src_points)

        def one_turn(turn, acc):
            begin = turn * step
            return acc + tile_terms(
                tgt_points,
                lax.dynamic_slice_in_dim(src_points, begin, step, 1),
                lax.dynamic_slice_in_dim(src_area, begin, step, 0),
                lax.dynamic_slice_in_dim(direct_cols, begin, step, 1),
                lax.dynamic_slice_in_dim(columns, begin, step, 1),
            )

        partial_sum = lax.fori_loop(0, turns, one_turn, empty)
        picked = jnp.take(gathered, near_index, axis=2)
        partial_sum = partial_sum + jnp.sum(picked * near_weight[None, None], axis=-1)
        summed = lax.psum_scatter(partial_sum, "col", scatter_dimension=2, tiled=True)
        image = self_term[None, None] * vector + summed
        for j in range(k + 1):
            value = lax.psum(jnp.sum(basis[j] * image, axis=(1, 2)), ("row", "col"))
            hessen[j, k] = value
            image = image - value[:, None, None] * basis[j]
        length = norm_of(image)
        hessen[k + 1, k] = length
        if k + 1 < ITERS:
            basis.append(image / length[:, None, None])
    coeffs = solve_small(hessen, start_norm, ITERS)
    density = coeffs[0][:, None, None] * basis[0]
    for k in range(1, ITERS):
        density = density + coeffs[k][:, None, None] * basis[k]
    return density


def solution(mesh):
    return jax.shard_map(
        body,
        mesh=mesh,
        in_specs=(
            P(None, None, ("row", "col")),
            P(None, ("row", "col")),
            P(("row", "col")),
            P(("row", "col")),
            P("row", "col"),
            P("row", "col"),
        ),
        out_specs=P(None, None, ("row", "col")),
        check_vma=False,
    )
```

profile of v0, /device:TPU:1, one launch (start us, length us, event | category | flops | bytes accessed | tf_op | source)
XLA Modules:
  0.0 1627.6 jit_solution(3706508605131403836)
XLA Ops:
  0.8 81.4 %psum.70 = f32[6]{0:T(128)S(1)} all-reduce(f32[6]{0:T(128)S(1)} %multiply_reduce_fusion.21), channel_id=1, replica_groups=mesh['row'=32,'col'=8] {'row','col'}, use_global_device_ids=true, to_apply=%region_1.0 | all-reduce | flops 6 | bytes 48 | tf_op jit(solution)/shard_map/psum | solution.py:99
  83.2 53.2 %all_gather.18 = f32[6,3,2048]{0,1,2:T(4,128)} all-gather(f32[6,3,64]{0,1,2:T(4,128)S(1)} %copy.171), channel_id=1, replica_groups=mesh['row'=32,'col'=8] {'row'}, dimensions={2}, use_global_device_ids=true | all-gather | bytes 152064 | tf_op jit(solution)/shard_map/all_gather | solution.py:106
  136.4 37.4 %all-gather.1 = f32[32,64,3]{1,2,0:T(4,128)S(1)} all-gather(f32[1,64,3]{1,2,0:T(4,128)S(1)} %bitcast.33), channel_id=1, replica_groups=mesh['row'=32,'col'=8] {'row'}, dimensions={0}, use_global_device_ids=true | all-gather | bytes 25344 | tf_op jit(solution)/shard_map/all_gather | solution.py:91
  205.8 19.2 %all-gather = f32[8,64,3]{1,2,0:T(4,128)S(1)} all-gather(f32[1,64,3]{1,2,0:T(4,128)S(1)} %bitcast.34), channel_id=1, replica_groups=mesh['row'=32,'col'=8] {'col'}, dimensions={0}, use_global_device_ids=true | all-gather | bytes 6912 | tf_op jit(solution)/shard_map/all_gather | solution.py:89
  226.6 70.3 %all-reduce = f32[2048]{0:T(1024)S(1)} all-reduce(f32[2048]{0:T(1024)S(1)} %dynamic-update-slice), channel_id=1, replica_groups=mesh['row'=32,'col'=8] {'row'}, use_global_device_ids=true, to_apply=%add | all-reduce | flops 2048 | bytes 16384
  296.9 18.5 %while.42 = (s32[]{:T(128)}, f32[6,3,512]{2,1,0:T(4,128)}, f32[18,2048]{1,0:T(8,128)}, f32[3,512]{1,0:T(4,128)S(1)}, f32[3,2048]{1,0:T(4,128)S(1)}, /*index=5*/f...) while((s32[]{:T(128)}, f32[6,3,512]{2,1,0:T(4,128)}, ...), condition=%wide.region_7.0_spmd.clone, body=%wide.region_3.0_spmd.clone.sunk | while | flops 727831552 | bytes 12562725 | solution.py:122
  316.4 62.0 %gather_fusion = f32[8192,6,3]{1,2,0:T(4,128)} fusion(f32[6,3,2048]{0,1,2:T(4,128)} %all_gather.18, s32[8192]{0:T(1024)S(1)} %broadcast_clamp_fusion), kind=kCustom, calls=%fused_computation.clone | custom fusion | bytes 1212416 | tf_op jit(solution)/shard_map/jit(_take)/gather | solution.py:123
  399.8 53.8 %all-reduce.1 = f32[6,3,512]{0,1,2:T(4,128)} all-reduce(f32[6,3,512]{0,1,2:T(4,128)S(1)} %copy.184), channel_id=2, replica_groups=mesh['row'=32,'col'=8] {'col'}, use_global_device_ids=true, to_apply=%region_9.11.clone | all-reduce | flops 9216 | bytes 73728
  456.1 85.6 %psum.71 = f32[6]{0:T(128)S(1)} all-reduce(f32[6]{0:T(128)S(1)} %multiply_reduce_fusion.20), channel_id=1, replica_groups=mesh['row'=32,'col'=8] {'row','col'}, use_global_device_ids=true, to_apply=%region_11.13 | all-reduce | flops 6 | bytes 48 | tf_op jit(solution)/shard_map/psum | solution.py:128
  541.9 73.2 %psum.72 = f32[6]{0:T(128)S(1)} all-reduce(f32[6]{0:T(128)S(1)} %multiply_reduce_fusion.19), channel_id=1, replica_groups=mesh['row'=32,'col'=8] {'row','col'}, use_global_device_ids=true, to_apply=%region_13.15 | all-reduce | flops 6 | bytes 48 | tf_op jit(solution)/shard_map/psum | solution.py:99
  615.3 51.1 %all_gather.22 = f32[6,3,2048]{0,1,2:T(4,128)S(1)} all-gather(f32[6,3,64]{0,1,2:T(4,128)S(1)} %copy.186), channel_id=1, replica_groups=mesh['row'=32,'col'=8] {'row'}, dimensions={2}, use_global_device_ids=true | all-gather | bytes 152064 | tf_op jit(solution)/shard_map/all_gather | solution.py:106
  697.2 20.2 %while.43 = (s32[]{:T(128)}, f32[6,3,512]{2,1,0:T(4,128)}, f32[18,2048]{1,0:T(8,128)}, f32[3,512]{1,0:T(4,128)S(1)}, f32[3,2048]{1,0:T(4,128)S(1)}, /*index=5*/f...) while((s32[]{:T(128)}, f32[6,3,512]{2,1,0:T(4,128)}, ...), condition=%wide.region_19.0_spmd.clone, body=%wide.region_15.20_spmd.clone.sunk | while | flops 727831552 | bytes 12579137 | solution.py:122
  717.5 62.0 %gather_fusion.1 = f32[8192,6,3]{1,2,0:T(4,128)} fusion(f32[6,3,2048]{0,1,2:T(4,128)} %copy-done.1, s32[8192]{0:T(1024)S(1)} %broadcast_clamp_fusion), kind=kCustom, calls=%fused_computation.1.clone | custom fusion | bytes 1212416 | tf_op jit(solution)/shard_map/jit(_take)/gather | solution.py:123
  800.6 54.3 %all-reduce.2 = f32[6,3,512]{0,1,2:T(4,128)} all-reduce(f32[6,3,512]{0,1,2:T(4,128)S(1)} %copy.195), channel_id=3, replica_groups=mesh['row'=32,'col'=8] {'col'}, use_global_device_ids=true, to_apply=%region_21.23.clone | all-reduce | flops 9216 | bytes 73728
  856.1 85.6 %psum.73 = f32[6]{0:T(128)S(1)} all-reduce(f32[6]{0:T(128)S(1)} %multiply_reduce_fusion.18), channel_id=1, replica_groups=mesh['row'=32,'col'=8] {'row','col'}, use_global_device_ids=true, to_apply=%region_23.25 | all-reduce | flops 6 | bytes 48 | tf_op jit(solution)/shard_map/psum | solution.py:128
  941.9 73.3 %psum.74 = f32[6]{0:T(128)S(1)} all-reduce(f32[6]{0:T(128)S(1)} %multiply_reduce_fusion.17), channel_id=1, replica_groups=mesh['row'=32,'col'=8] {'row','col'}, use_global_device_ids=true, to_apply=%region_25.27 | all-reduce | flops 6 | bytes 48 | tf_op jit(solution)/shard_map/psum | solution.py:128
  1015.4 73.1 %psum.75 = f32[6]{0:T(128)S(1)} all-reduce(f32[6]{0:T(128)S(1)} %get-tuple-element.503), channel_id=1, replica_groups=mesh['row'=32,'col'=8] {'row','col'}, use_global_device_ids=true, to_apply=%region_27.29 | all-reduce | flops 6 | bytes 48 | tf_op jit(solution)/shard_map/psum | solution.py:99
  1089.3 52.3 %all_gather.23 = f32[6,3,2048]{0,1,2:T(4,128)S(1)} all-gather(f32[6,3,64]{0,1,2:T(4,128)S(1)} %copy.197), channel_id=1, replica_groups=mesh['row'=32,'col'=8] {'row'}, dimensions={2}, use_global_device_ids=true | all-gather | bytes 152064 | tf_op jit(solution)/shard_map/all_gather | solution.py:106
  1182.9 62.0 %gather_fusion.2 = f32[8192,6,3]{1,2,0:T(4,128)} fusion(f32[6,3,2048]{0,1,2:T(4,128)} %copy-done, s32[8192]{0:T(1024)S(1)} %broadcast_clamp_fusion), kind=kCustom, calls=%fused_computation.2.clone | custom fusion | bytes 1212416 | tf_op jit(solution)/shard_map/jit(_take)/gather | solution.py:123
  1265.9 54.5 %all-reduce.3 = f32[6,3,512]{0,1,2:T(4,128)S(1)} all-reduce(f32[6,3,512]{0,1,2:T(4,128)S(1)} %copy.206), channel_id=4, replica_groups=mesh['row'=32,'col'=8] {'col'}, use_global_device_ids=true, to_apply=%region_35.37.clone | all-reduce | flops 9216 | bytes 73728
  1320.7 85.0 %psum.76 = f32[6]{0:T(128)S(1)} all-reduce(f32[6]{0:T(128)S(1)} %multiply_reduce_fusion.15), channel_id=1, replica_groups=mesh['row'=32,'col'=8] {'row','col'}, use_global_device_ids=true, to_apply=%region_37.39 | all-reduce | flops 6 | bytes 48 | tf_op jit(solution)/shard_map/psum | solution.py:128
  1405.9 73.2 %psum.77 = f32[6]{0:T(128)S(1)} all-reduce(f32[6]{0:T(128)S(1)} %get-tuple-element.501), channel_id=1, replica_groups=mesh['row'=32,'col'=8] {'row','col'}, use_global_device_ids=true, to_apply=%region_39.41 | all-reduce | flops 6 | bytes 48 | tf_op jit(solution)/shard_map/psum | solution.py:128
  1479.3 72.9 %psum.78 = f32[6]{0:T(128)S(1)} all-reduce(f32[6]{0:T(128)S(1)} %multiply_reduce_fusion.13), channel_id=1, replica_groups=mesh['row'=32,'col'=8] {'row','col'}, use_global_device_ids=true, to_apply=%region_41.43 | all-reduce | flops 6 | bytes 48 | tf_op jit(solution)/shard_map/psum | solution.py:128
  1552.4 74.2 %psum.79 = f32[6]{0:T(128)S(1)} all-reduce(f32[6]{0:T(128)S(1)} %multiply_reduce_fusion.12), channel_id=1, replica_groups=mesh['row'=32,'col'=8] {'row','col'}, use_global_device_ids=true, to_apply=%region_43.45 | all-reduce | flops 6 | bytes 48 | tf_op jit(solution)/shard_map/psum | solution.py:99
  (293 shorter events, 227.8 us)
Async XLA Ops:
  82.2 532.8 %copy-start.23 = (f32[6]{0:T(128)}, f32[6]{0:T(128)S(1)}, u32[]{:S(2)}) copy-start(f32[6]{0:T(128)S(1)} %sqrt.21) | copy-start | bytes 76
  83.2 53.3 %copy-start.30 = (f32[3,64]{1,0:T(4,128)S(1)}, f32[3,64]{1,0:T(4,128)}, u32[]{:S(2)}) copy-start(f32[3,64]{1,0:T(4,128)} %param.15) | copy-start | bytes 2308
  202.8 22.3 %copy-start.45 = (u32[256]{0:T(256)S(1)}, u32[256]{0:T(256)}, u32[]{:S(2)}) copy-start(u32[256]{0:T(256)} %constant.177) | copy-start | bytes 3076
  202.8 23.5 %copy-start.43 = (f32[64]{0:T(128)S(1)}, f32[64]{0:T(128)}, u32[]{:S(2)}) copy-start(f32[64]{0:T(128)} %param.16) | copy-start | bytes 772
  399.4 54.2 %copy-start.44 = (u32[256]{0:T(256)S(1)}, u32[256]{0:T(256)}, u32[]{:S(2)}) copy-start(u32[256]{0:T(256)} %constant.183) | copy-start | bytes 3076
  399.4 56.5 %copy-start.12 = (f32[6,3,64]{2,1,0:T(4,128)S(1)}, f32[6,3,64]{2,1,0:T(4,128)}, u32[]{:S(2)}) copy-start(f32[6,3,64]{2,1,0:T(4,128)} %param.14) | copy-start | bytes 13828
  399.4 56.5 %copy-start.25 = (f32[64]{0:T(128)S(1)}, f32[64]{0:T(128)}, u32[]{:S(2)}) copy-start(f32[64]{0:T(128)} %param.17) | copy-start | bytes 772
  541.7 124.8 %copy-start.31 = (f32[6]{0:T(128)}, f32[6]{0:T(128)S(1)}, u32[]{:S(2)}) copy-start(f32[6]{0:T(128)S(1)} %psum.71) | copy-start | bytes 76
  615.1 51.4 %copy-start.37 = (f32[6]{0:T(128)}, f32[6]{0:T(128)S(1)}, u32[]{:S(2)}) copy-start(f32[6]{0:T(128)S(1)} %psum.72) | copy-start | bytes 76
  615.2 51.3 %copy-start.16 = (f32[6,3,64]{2,0,1:T(8,128)}, f32[6,3,64]{2,0,1:T(8,128)S(1)}, u32[]{:S(2)}) copy-start(f32[6,3,64]{2,0,1:T(8,128)S(1)} %broadcast_divide_fusion.1) | copy-start | bytes 13828
  800.1 55.8 %copy-start.13 = (f32[6,3,64]{2,1,0:T(4,128)S(1)}, f32[6,3,64]{2,1,0:T(4,128)}, u32[]{:S(2)}) copy-start(f32[6,3,64]{2,1,0:T(4,128)} %param.14) | copy-start | bytes 13828
  800.1 55.8 %copy-start.17 = (f32[6,3,64]{2,0,1:T(8,128)S(1)}, f32[6,3,64]{2,0,1:T(8,128)}, u32[]{:S(2)}) copy-start(f32[6,3,64]{2,0,1:T(8,128)} %copy-done.16) | copy-start | bytes 13828
  800.1 55.8 %copy-start.24 = (f32[6]{0:T(128)S(1)}, f32[6]{0:T(128)}, u32[]{:S(2)}) copy-start(f32[6]{0:T(128)} %copy-done.23) | copy-start | bytes 76
  800.1 55.8 %copy-start.26 = (f32[64]{0:T(128)S(1)}, f32[64]{0:T(128)}, u32[]{:S(2)}) copy-start(f32[64]{0:T(128)} %param.17) | copy-start | bytes 772
  941.7 73.7 %copy-start.33 = (f32[6]{0:T(128)}, f32[6]{0:T(128)S(1)}, u32[]{:S(2)}) copy-start(f32[6]{0:T(128)S(1)} %psum.73) | copy-start | bytes 76
  1015.2 126.4 %copy-start.35 = (f32[6]{0:T(128)}, f32[6]{0:T(128)S(1)}, u32[]{:S(2)}) copy-start(f32[6]{0:T(128)S(1)} %psum.74) | copy-start | bytes 76
  1089.1 52.6 %copy-start.28 = (f32[6]{0:T(128)}, f32[6]{0:T(128)S(1)}, u32[]{:S(2)}) copy-start(f32[6]{0:T(128)S(1)} %sqrt.24) | copy-start | bytes 76
  1265.4 55.1 %copy-start.29 = (f32[6]{0:T(128)S(1)}, f32[6]{0:T(128)}, u32[]{:S(2)}) copy-start(f32[6]{0:T(128)} %copy-done.28) | copy-start | bytes 76
  1265.4 361.1 %copy-start.32 = (f32[6]{0:T(128)S(1)}, f32[6]{0:T(128)}, u32[]{:S(2)}) copy-start(f32[6]{0:T(128)} %copy-done.31) | copy-start | bytes 76
  1265.4 361.1 %copy-start.38 = (f32[6]{0:T(128)S(1)}, f32[6]{0:T(128)}, u32[]{:S(2)}) copy-start(f32[6]{0:T(128)} %copy-done.37) | copy-start | bytes 76
  1265.5 361.1 %copy-start.34 = (f32[6]{0:T(128)S(1)}, f32[6]{0:T(128)}, u32[]{:S(2)}) copy-start(f32[6]{0:T(128)} %copy-done.33) | copy-start | bytes 76
  1265.5 361.1 %copy-start.36 = (f32[6]{0:T(128)S(1)}, f32[6]{0:T(128)}, u32[]{:S(2)}) copy-start(f32[6]{0:T(128)} %copy-done.35) | copy-start | bytes 76
  1265.5 361.1 %copy-start.40 = (f32[6]{0:T(128)S(1)}, f32[6]{0:T(128)}, u32[]{:S(2)}) copy-start(f32[6]{0:T(128)} %copy-done.39) | copy-start | bytes 76
  1265.5 361.1 %copy-start.42 = (f32[6]{0:T(128)S(1)}, f32[6]{0:T(128)}, u32[]{:S(2)}) copy-start(f32[6]{0:T(128)} %copy-done.41) | copy-start | bytes 76
  (32 other events, 140.7 us)
where the time goes:
time: 1640 us; the launch traced here: 1630 us
  blocking collectives  1220 us (74%)
  local copies, waits for them, and re-layouts  283 us (17%)
  other arithmetic  86.7 us (5%)
  matrix products  31.7 us (2%)
    psum x6, blocking collectives, body(): value = lax.psum(jnp.sum(basis[j] * image, axis=(1, 2)), ('row', 'col'))  476 us
    psum x4, blocking collectives, norm_of(): lax.psum(jnp.sum(field * field, axis=(1, 2)), ('row', 'col'))  302 us
    gather x6, local copies, waits for them, and re-layouts, body(): picked = jnp.take(gathered, near_index, axis=2)  237 us
    unnamed x4, blocking collectives  233 us
    all_gather x3, blocking collectives, body(): gathered = lax.all_gather(vector, 'row', axis=2, tiled=True)  157 us
    all_gather x1, blocking collectives, body(): lax.all_gather(points, 'row', axis=1, tiled=True)  37.4 us
    reduce_sum x3, other arithmetic, build_columns(): inner_prod = jnp.sum(src_points[None] * values, axis=1)  35.1 us

commit v1 on v0

v1 whole, which is shorter than its diff:
```python
import functools
import math

import jax
import jax.numpy as jnp
from jax import lax
from jax.experimental import pallas as pl
from jax.experimental.pallas import tpu as pltpu
from jax.sharding import PartitionSpec as P

MESH = pl.DeviceIdType.MESH
ITERS = 3
BLOB_SQ = 0.0025
INV_EIGHT_PI = 1.0 / (8.0 * math.pi)
GROUP = 16
PAN = 64
LOCAL = GROUP * PAN
LISTED = 16
PAIRS = ((0, 0, 0), (1, 1, 1), (2, 2, 2), (0, 1, 3), (0, 2, 4), (1, 2, 5))
FAR_FIRST = (8, 9, 7, 6, 10, 5, 11, 4, 12, 3, 13, 2, 14, 1, 15)
CHUNK = 256
TILE = 128


def kernel(
    pkt0_ref,
    nidx_ref,
    nwt_ref,
    out_ref,
    pkt,
    ag,
    pts,
    rss,
    rsr,
    nidx,
    nwt,
    srcb,
    tgtb,
    nmat,
    wts,
    fld,
    ag_send,
    ag_recv,
    pts_send,
    pts_recv,
    rs_send,
    rs_recv,
    near_send,
    near_recv,
):
    row = lax.axis_index("row")
    col = lax.axis_index("col")
    y_hi = row // GROUP
    q = row % GROUP
    p = y_hi * 8 + col

    def gather_peer(d):
        other = (q + d) % GROUP
        return other, (y_hi * GROUP + other, col)

    def reduce_device(other):
        return ((other // 8) * GROUP + q, other % 8)

    barrier = pltpu.get_barrier_semaphore()
    for d in range(1, GROUP):
        pl.semaphore_signal(barrier, inc=1, device_id=gather_peer(d)[1], device_id_type=MESH)
        pl.semaphore_signal(barrier, inc=1, device_id=reduce_device((p + d) % GROUP), device_id_type=MESH)

    nidx[y_hi] = jnp.transpose(nidx_ref[...])
    nwt[y_hi] = jnp.transpose(nwt_ref[...])
    pl.semaphore_wait(barrier, 2 * (GROUP - 1))

    partner = ((1 - y_hi) * GROUP + q, col)

    def near_copies(slot):
        return [
            pltpu.make_async_remote_copy(
                src_ref=buf.at[slot],
                dst_ref=buf.at[slot],
                send_sem=near_send.at[i],
                recv_sem=near_recv.at[i],
                device_id=partner,
                device_id_type=MESH,
            )
            for i, buf in enumerate((nidx, nwt))
        ]

    def ag_copy(src, k, d, slot):
        return pltpu.make_async_remote_copy(
            src_ref=src,
            dst_ref=ag.at[k, slot],
            send_sem=ag_send.at[k, d],
            recv_sem=ag_recv.at[k, slot],
            device_id=gather_peer(d)[1],
            device_id_type=MESH,
        )

    def pts_copy(d, slot):
        return pltpu.make_async_remote_copy(
            src_ref=pkt0_ref,
            dst_ref=pts.at[slot],
            send_sem=pts_send.at[d],
            recv_sem=pts_recv.at[slot],
            device_id=reduce_device((p + d) % GROUP),
            device_id_type=MESH,
        )

    def rs_copy(k, other, slot, send_slot):
        return pltpu.make_async_remote_copy(
            src_ref=rss.at[k, other],
            dst_ref=rsr.at[k, slot],
            send_sem=rs_send.at[k, send_slot],
            recv_sem=rs_recv.at[k, slot],
            device_id=reduce_device(other),
            device_id_type=MESH,
        )

    for d in FAR_FIRST:
        ag_copy(pkt0_ref, 0, d, q).start()
        pts_copy(d, p).start()
    for copy in near_copies(y_hi):
        copy.start()
    ag[0, q] = pkt0_ref[...]
    pts[p] = pkt0_ref[...]

    def near_half(half):
        def one(step, carry):
            tile = step // 16
            rows = step % 16
            lanes = pl.ds(pl.multiple_of(tile * TILE, TILE), TILE)
            place = lax.broadcasted_iota(jnp.int32, (64, TILE), 0) + (rows * 64 + y_hi * LOCAL)
            acc = jnp.zeros((64, TILE), jnp.float32)
            for k in range(LISTED):
                idx = nidx[half, pl.ds(k, 1), lanes]
                wt = nwt[half, pl.ds(k, 1), lanes]
                acc = acc + jnp.where(place == idx, wt, 0.0)
            nmat[
                pl.ds(pl.multiple_of(rows * 64, 64), 64),
                pl.ds(pl.multiple_of(half * 512 + tile * TILE, TILE), TILE),
            ] = acc
            return carry

        lax.fori_loop(0, 64, one, 0)

    near_half(y_hi)
    for copy in near_copies(1 - y_hi):
        copy.wait_recv()
    near_half(1 - y_hi)

    lane = lax.broadcasted_iota(jnp.int32, (8, TILE), 1)
    low = lane < PAN
    wide = lax.broadcasted_iota(jnp.int32, (8, 2 * TILE), 1)
    body_lanes = wide < 3 * PAN

    def swap(x):
        return pltpu.roll(x, PAN, 1)

    def join(first, second):
        a, c = first[:, :TILE], first[:, TILE:]
        b, e = second[:, :TILE], second[:, TILE:]
        return (
            jnp.where(low, a, swap(b)),
            jnp.where(low, swap(a), b),
            jnp.where(low, c, swap(e)),
        )

    def wait_gather(k):
        for d in range(1, GROUP):
            other = (q + d) % GROUP
            ag_copy(pkt0_ref, k, d, other).wait_recv()

    wait_gather(0)
    for d in range(1, GROUP):
        pts_copy(d, (p + d) % GROUP).wait_recv()

    for s in range(GROUP):
        for half in range(2):
            line = ag[0, s, 6:7, half * TILE : (half + 1) * TILE]
            flipped = jnp.transpose(jnp.broadcast_to(line, (TILE, TILE)))
            if half == 0:
                srcb[0, s * PAN : (s + 1) * PAN] = flipped[:PAN]
                srcb[1, s * PAN : (s + 1) * PAN] = flipped[PAN:]
            else:
                srcb[2, s * PAN : (s + 1) * PAN] = flipped[:PAN]
                srcb[3, s * PAN : (s + 1) * PAN] = flipped[PAN:] * INV_EIGHT_PI
    for m in range(GROUP // 2):
        for a, tile in enumerate(join(pts[2 * m], pts[2 * m + 1])):
            tgtb[a, :, m * TILE : (m + 1) * TILE] = jnp.broadcast_to(tile[6:7], (16, TILE))

    def build(chunk):
        def one(step, carry):
            rows = pl.ds(pl.multiple_of(step * 16, 16), 16)
            source = [srcb[i, rows, :] for i in range(4)]
            for t in range(CHUNK // TILE):
                lanes = pl.ds(pl.multiple_of(chunk * CHUNK + t * TILE, TILE), TILE)
                off = [tgtb[a, :, lanes] - source[a] for a in range(3)]
                dist = off[0] * off[0] + off[1] * off[1] + off[2] * off[2]
                inv = lax.rsqrt(dist + BLOB_SQ)
                two = source[3] * inv * inv * inv
                one_near = (dist + 2.0 * BLOB_SQ) * two + nmat[rows, lanes]
                scaled = [two * v for v in off]
                for a, b, block in PAIRS:
                    value = scaled[a] * off[b]
                    if a == b:
                        value = value + one_near
                    high = value.astype(jnp.bfloat16)
                    wts[block, 0, rows, lanes] = high
                    wts[block, 1, rows, lanes] = (value - high.astype(jnp.float32)).astype(jnp.bfloat16)
            return carry

        lax.fori_loop(0, LOCAL // 16, one, 0)

    def fill_fields(k):
        for m in range(GROUP // 2):
            for a, tile in enumerate(join(ag[k, 2 * m], ag[k, 2 * m + 1])):
                high = tile.astype(jnp.bfloat16).astype(jnp.float32)
                fld[a, :, m * TILE : (m + 1) * TILE] = jnp.concatenate([high, tile - high], axis=0).astype(jnp.bfloat16)

    def group_dots(k):
        if k == 0:
            total = jnp.zeros((8, 2 * TILE), jnp.float32)
            for s in range(GROUP):
                total = total + ag[0, s] * ag[0, s]
            return jnp.broadcast_to(jnp.sum(jnp.where(body_lanes, total, 0.0), axis=1, keepdims=True), (8, TILE))
        total = ag[k, 0, :, TILE:]
        for s in range(1, GROUP):
            total = total + ag[k, s, :, TILE:]
        return total

    def apply(k):
        fill_fields(k)
        riding = group_dots(k)

        def one(step, carry):
            chunk = (p // 4 + 1 + step) % 4
            if k == 0:
                build(chunk)
            lanes = pl.ds(pl.multiple_of(chunk * CHUNK, CHUNK), CHUNK)
            acc = [jnp.zeros((16, CHUNK), jnp.float32) for _ in range(3)]
            for a, b, block in PAIRS:
                for part in range(2):
                    weights = wts[block, part, :, lanes]
                    if a == b:
                        acc[a] = acc[a] + jnp.dot(fld[a], weights, preferred_element_type=jnp.float32)
                    else:
                        both = jnp.dot(
                            jnp.concatenate([fld[a], fld[b]], axis=0), weights, preferred_element_type=jnp.float32
                        )
                        acc[b] = acc[b] + both[:16]
                        acc[a] = acc[a] + both[16:]
            sums = [v[:8] + v[8:] for v in acc]
            for i in range(4):
                t, odd = i // 2, i % 2
                first, second, third = [v[:, t * TILE : (t + 1) * TILE] for v in sums]
                if odd:
                    first, third = swap(first), swap(third)
                else:
                    second = swap(second)
                other = chunk * 4 + i
                rss[k, other, :, :TILE] = jnp.where(low, first, second)
                rss[k, other, :, TILE:] = jnp.where(low, third, riding)

                @pl.when(other != p)
                def _():
                    rs_copy(k, other, p, other).start()

            return carry

        lax.fori_loop(0, 4, one, 0)
        return collect(k)

    def collect(k):
        total = rss[k, p]
        for d in range(1, GROUP):
            other = (p + d) % GROUP
            rs_copy(k, other, other, other).wait_recv()
            total = total + rsr[k, other]
        return total

    def send_packet(k, vector, dots):
        value = jnp.where(body_lanes, vector, 0.0)
        for i, dot in enumerate(dots):
            value = jnp.where(wide == 3 * PAN + i, dot, value)
        pkt[k] = value
        ag[k, q] = value
        for d in FAR_FIRST:
            ag_copy(pkt.at[k], k, d, q).start()

    def inner(a, b):
        return jnp.sum(jnp.where(body_lanes, a * b, 0.0), axis=1, keepdims=True)

    def pick(total, i):
        return total[:, 3 * PAN + i : 3 * PAN + i + 1]

    def length_of(square, whole):
        return jnp.sqrt(jnp.maximum(square, whole * 1e-7))

    own = jnp.where(body_lanes, pkt0_ref[...], 0.0)
    self_term = jnp.broadcast_to(jnp.where(body_lanes, pkt0_ref[...], 0.0)[7:8], (8, 2 * TILE))

    total = apply(0)
    start_norm = jnp.sqrt(pick(total, 0))
    basis0 = own / start_norm
    image0 = (self_term * own + total) / start_norm

    send_packet(1, image0, [inner(basis0, image0), inner(image0, image0)])
    wait_gather(1)
    total = apply(1)
    h00 = pick(total, 0)
    square = pick(total, 1)
    h10 = length_of(square - h00 * h00, square)
    basis1 = (image0 - h00 * basis0) / h10
    image1 = (self_term * image0 + total - h00 * image0) / h10

    send_packet(
        2,
        image1,
        [inner(basis1, basis1), inner(basis0, image1), inner(basis1, image1), inner(image1, image1)],
    )
    wait_gather(2)
    total = apply(2)
    scale = jnp.sqrt(pick(total, 0))
    second_image = (self_term * image1 + total) / scale
    basis1 = basis1 / scale
    image1 = image1 / scale
    h10 = h10 * scale
    h01 = pick(total, 1) / scale
    h11 = pick(total, 2) / (scale * scale)
    square = pick(total, 3) / (scale * scale)
    h21 = length_of(square - h01 * h01 - h11 * h11, square)
    basis2 = (image1 - h01 * basis0 - h11 * basis1) / h21
    image2 = (second_image - h01 * image0 - h11 * image1) / h21

    send_packet(
        3,
        image2,
        [
            inner(basis2, basis2),
            inner(basis0, image2),
            inner(basis1, image2),
            inner(basis2, image2),
            inner(image2, image2),
        ],
    )
    wait_gather(3)
    riding = group_dots(3)
    for d in range(GROUP):
        rss[3, d, :, TILE:] = riding
        rss[3, d, :, :TILE] = riding
    for d in FAR_FIRST:
        other = (p + d) % GROUP
        rs_copy(3, other, p, other).start()
    total = collect(3)
    scale = jnp.sqrt(pick(total, 0))
    basis2 = basis2 / scale
    h21 = h21 * scale
    h02 = pick(total, 1) / scale
    h12 = pick(total, 2) / scale
    h22 = pick(total, 3) / (scale * scale)
    square = pick(total, 4) / (scale * scale)
    h32 = jnp.sqrt(jnp.maximum(square - h02 * h02 - h12 * h12 - h22 * h22, 0.0))

    columns = [[h00, h10], [h01, h11, h21], [h02, h12, h22, h32]]
    target = [start_norm] + [jnp.zeros_like(start_norm)] * ITERS
    turns = []
    for k in range(ITERS):
        column = columns[k]
        for j in range(k):
            cosine, sine = turns[j]
            column[j], column[j + 1] = (
                cosine * column[j] + sine * column[j + 1],
                cosine * column[j + 1] - sine * column[j],
            )
        radius = jnp.sqrt(column[k] * column[k] + column[k + 1] * column[k + 1])
        cosine, sine = column[k] / radius, column[k + 1] / radius
        turns.append((cosine, sine))
        column[k] = radius
        target[k + 1] = -sine * target[k]
        target[k] = cosine * target[k]
    coeffs = [None] * ITERS
    for k in range(ITERS - 1, -1, -1):
        accum = target[k]
        for i in range(k + 1, ITERS):
            accum = accum - columns[i][k] * coeffs[i]
        coeffs[k] = accum / columns[k][k]
    out_ref[...] = coeffs[0] * basis0 + coeffs[1] * basis1 + coeffs[2] * basis2

    for copy in near_copies(y_hi):
        copy.wait_send()
    for d in range(1, GROUP):
        ag_copy(pkt0_ref, 0, d, q).wait_send()
        pts_copy(d, p).wait_send()
        for k in range(1, ITERS + 1):
            ag_copy(pkt.at[k], k, d, q).wait_send()
        for k in range(ITERS + 1):
            other = (p + d) % GROUP
            rs_copy(k, other, p, other).wait_send()


def body(velocity, points, panel_area, self_term, near_index, near_weight):
    rhs = velocity.shape[0]
    top = jnp.pad(velocity.reshape(rhs, 3 * PAN), ((0, 0), (0, PAN)))
    places = jnp.concatenate([points.reshape(1, 3 * PAN), panel_area.reshape(1, PAN)], axis=1)
    own = jnp.concatenate([self_term] * 4).reshape(1, 4 * PAN)
    packet = jnp.concatenate([top, places, own], axis=0)
    rounds = ITERS + 1
    vmem = pl.BlockSpec(memory_space=pltpu.VMEM)
    result = pl.pallas_call(
        kernel,
        out_shape=jax.ShapeDtypeStruct((8, 4 * PAN), jnp.float32),
        in_specs=[vmem] * 3,
        out_specs=vmem,
        scratch_shapes=[
            pltpu.VMEM((rounds, 8, 4 * PAN), jnp.float32),
            pltpu.VMEM((rounds, GROUP, 8, 4 * PAN), jnp.float32),
            pltpu.VMEM((GROUP, 8, 4 * PAN), jnp.float32),
            pltpu.VMEM((rounds, GROUP, 8, 4 * PAN), jnp.float32),
            pltpu.VMEM((rounds, GROUP, 8, 4 * PAN), jnp.float32),
            pltpu.VMEM((2, LISTED, 512), jnp.int32),
            pltpu.VMEM((2, LISTED, 512), jnp.float32),
            pltpu.VMEM((4, LOCAL, TILE), jnp.float32),
            pltpu.VMEM((3, 16, LOCAL), jnp.float32),
            pltpu.VMEM((LOCAL, LOCAL), jnp.float32),
            pltpu.VMEM((6, 2, LOCAL, LOCAL), jnp.bfloat16),
            pltpu.VMEM((3, 16, LOCAL), jnp.bfloat16),
            pltpu.SemaphoreType.DMA((rounds, GROUP)),
            pltpu.SemaphoreType.DMA((rounds, GROUP)),
            pltpu.SemaphoreType.DMA((GROUP,)),
            pltpu.SemaphoreType.DMA((GROUP,)),
            pltpu.SemaphoreType.DMA((rounds, GROUP)),
            pltpu.SemaphoreType.DMA((rounds, GROUP)),
            pltpu.SemaphoreType.DMA((2,)),
            pltpu.SemaphoreType.DMA((2,)),
        ],
        compiler_params=pltpu.CompilerParams(
            collective_id=0, has_side_effects=True, vmem_limit_bytes=56 * 1024 * 1024
        ),
    )(packet, near_index, near_weight)
    return result[:rhs, : 3 * PAN].reshape(rhs, 3, PAN)


def solution(mesh):
    return jax.shard_map(
        body,
        mesh=mesh,
        in_specs=(
            P(None, None, ("row", "col")),
            P(None, ("row", "col")),
            P(("row", "col")),
            P(("row", "col")),
            P("row", "col"),
            P("row", "col"),
        ),
        out_specs=P(None, None, ("row", "col")),
        check_vma=False,
    )
```

time: 1640 us -> 89.1 us (0.05)
  blocking collectives: 1220 us -> 0 us
  local copies, waits for them, and re-layouts: 283 us -> 4.58 us
  other arithmetic: 86.7 us -> 2.21 us
  Pallas kernels: 0 us -> 82 us
  matrix products: 31.7 us -> 0 us
    psum x10 -> x0, blocking collectives: 777 us -> none  [the longest x6 476 us: body(): value = lax.psum(jnp.sum(basis[j] * image, axis=(1, 2)), ('row', 'col'))]
    gather x6 -> x0, local copies, waits for them, and re-layouts: 237 us -> none  [body(): picked = jnp.take(gathered, near_index, axis=2)]
    unnamed x4 -> x0, blocking collectives: 233 us -> none
    all_gather x5 -> x0, blocking collectives: 213 us -> none  [the longest x3 157 us: body(): gathered = lax.all_gather(vector, 'row', axis=2, tiled=True)]
    pallas_call x0 -> x1, Pallas kernels: none -> 82 us  [body(): pl.pallas_call(kernel, out_shape=jax.ShapeDtypeStruct((8, 4 * PAN), jnp.f...]
    reduce_sum x34 -> x0, other arithmetic: 53.4 us -> none  [the longest x3 35.1 us: build_columns(): inner_prod = jnp.sum(src_points[None] * values, axis=1)]
    dot_general x12 -> x0, matrix products: 31.7 us -> none  [the longest x6 17.1 us: tile_terms(): lax.dot_general(direct_cols, kernel_one, dims, precision=lax.Precision.HI...]
    mul x6 -> x0, other arithmetic: 26.4 us -> none  [the longest x3 26 us: build_columns(): src_points[None] * inner_prod[:, None]]
where the time goes in v1:
time: 89.1 us; the launch traced here: 88.8 us
  Pallas kernels  82 us (92%)
  local copies, waits for them, and re-layouts  4.58 us (5%)
  other arithmetic  2.21 us (2%)
    pallas_call x1, Pallas kernels, body(): pl.pallas_call(kernel, out_shape=jax.ShapeDtypeStruct((8, 4 * PAN), jnp.f...  82 us

profile of v1, /device:TPU:1, one launch (start us, length us, event | category | flops | bytes accessed | tf_op | source)
XLA Modules:
  0.0 88.8 jit_solution(15693799054126915961)
XLA Ops:
  0.0 0.0 copy-start
  0.0 0.8 reshape.16
  0.8 0.9 pad_maximum_fusion
  1.6 0.8 reshape.15
  2.4 1.3 %fusion.pkt0_ref = f32[8,256]{1,0:T(8,128)} fusion(f32[6,192]{1,0:T(8,128)S(1)} %reshape.15, f32[1,256]{1,0:T(1,128)S(1)} %bitcast.4, f32[1,64]{1,0:T(1,128)} %bitcast.5, f32[1,192]{1,0:T(1,128)S(1)} %reshape.16), kind=kLoop, calls=%fused_computation.1 | loop fusion | flops 10240 | bytes 14848 | tf_op jit(solution)/shard_map/concatenate | solution.py:405
  3.8 0.0 copy-done
  3.8 0.0 copy-start.1
  3.8 0.8 copy.7.nidx_ref
  4.6 0.0 copy-done.1
  4.6 0.8 copy.8.nwt_ref
  5.4 82.0 %shard_map.64 = f32[8,256]{1,0:T(8,128)} custom-call(f32[8,256]{1,0:T(8,128)} %fusion.pkt0_ref, s32[512,16]{1,0:T(8,128)} %copy.7.nidx_ref, f32[512,16]{1,0:T(8,128)} %copy.8.nwt_ref), custom_call_target="tpu_custom_call" | custom-call | tf_op jit(solution)/shard_map/pallas_call | solution.py:408
  87.5 1.4 %reshape.19 = f32[6,3,64]{2,1,0:T(4,128)} reshape(f32[6,192]{1,0:T(8,128)} %bitcast.3) | data formatting | bytes 9216 | tf_op jit(solution)/shard_map/reshape | solution.py:439
Async XLA Ops:
  0.0 3.8 %copy-start = (s32[512,16]{0,1:T(8,128)S(1)}, s32[512,16]{0,1:T(8,128)}, u32[]{:S(2)}) copy-start(s32[512,16]{0,1:T(8,128)} %param.10) | copy-start | bytes 98308
  3.8 0.8 copy-start.1

commit v2 on v1

v2 whole, which is shorter than its diff:
```python
import functools
import math

import jax
import jax.numpy as jnp
from jax import lax
from jax.experimental import pallas as pl
from jax.experimental.pallas import tpu as pltpu
from jax.sharding import PartitionSpec as P

MESH = pl.DeviceIdType.MESH
ITERS = 3
BLOB_SQ = 0.0025
INV_EIGHT_PI = 1.0 / (8.0 * math.pi)
GROUP = 16
PAN = 64
LOCAL = GROUP * PAN
LISTED = 16
MIXED = ((0, 1, 5), (0, 2, 6), (1, 2, 7))
BLOCKS = 8
FAR_FIRST = (8, 9, 7, 6, 10, 5, 11, 4, 12, 3, 13, 2, 14, 1, 15)
CHUNK = 256
TILE = 128
ROUNDS = ITERS + 1
EARLY = 3


def kernel(
    vel_ref,
    points_ref,
    area_ref,
    self_ref,
    nidx_ref,
    nwt_ref,
    out_ref,
    pkt,
    ag,
    pts,
    rss,
    rsr,
    far_idx,
    far_wt,
    digit_a,
    digit_b,
    srcb,
    tgtb,
    nmat,
    wts,
    uacc,
    ag_send,
    ag_recv,
    pts_send,
    pts_recv,
    rs_send,
    rs_recv,
    near_send,
    near_recv,
):
    row = lax.axis_index("row")
    col = lax.axis_index("col")
    y_hi = row // GROUP
    q = row % GROUP
    p = y_hi * 8 + col
    own_rows = q // 4
    own_lanes = p // 4

    def gather_device(other):
        return (y_hi * GROUP + other, col)

    def reduce_device(other):
        return ((other // 8) * GROUP + q, other % 8)

    barrier = pltpu.get_barrier_semaphore()
    for d in range(1, GROUP):
        pl.semaphore_signal(barrier, inc=1, device_id=gather_device((q + d) % GROUP), device_id_type=MESH)
        pl.semaphore_signal(barrier, inc=1, device_id=reduce_device((p + d) % GROUP), device_id_type=MESH)

    pkt[0] = jnp.zeros((8, 2 * TILE), jnp.float32)
    pkt[0, :6, :TILE] = jnp.concatenate([vel_ref[:, 0, :], vel_ref[:, 1, :]], axis=1)
    pkt[0, :6, TILE:] = jnp.concatenate([vel_ref[:, 2, :], jnp.zeros((6, PAN), jnp.float32)], axis=1)
    pkt[0, 6:7, :TILE] = jnp.concatenate([points_ref[0:1], points_ref[1:2]], axis=1)
    pkt[0, 6:7, TILE:] = jnp.concatenate([points_ref[2:3], area_ref[...]], axis=1)

    partner = ((1 - y_hi) * GROUP + q, col)

    def near_copies():
        return [
            pltpu.make_async_remote_copy(
                src_ref=mine,
                dst_ref=theirs,
                send_sem=near_send.at[i],
                recv_sem=near_recv.at[i],
                device_id=partner,
                device_id_type=MESH,
            )
            for i, (mine, theirs) in enumerate(((nidx_ref, far_idx), (nwt_ref, far_wt)))
        ]

    def window(ref, k):
        return ref if k < ITERS else ref.at[:, pl.ds(TILE, TILE)]

    def ag_copy(k, d, slot):
        return pltpu.make_async_remote_copy(
            src_ref=window(pkt.at[k], k),
            dst_ref=window(ag.at[k, slot], k),
            send_sem=ag_send.at[k, d],
            recv_sem=ag_recv.at[k, slot],
            device_id=gather_device((q + d) % GROUP),
            device_id_type=MESH,
        )

    def pts_copy(d, slot):
        return pltpu.make_async_remote_copy(
            src_ref=pkt.at[0],
            dst_ref=pts.at[slot],
            send_sem=pts_send.at[d],
            recv_sem=pts_recv.at[slot],
            device_id=reduce_device((p + d) % GROUP),
            device_id_type=MESH,
        )

    def rs_copy(k, other, slot):
        return pltpu.make_async_remote_copy(
            src_ref=window(rss.at[k, other], k),
            dst_ref=window(rsr.at[k, slot], k),
            send_sem=rs_send.at[k, other],
            recv_sem=rs_recv.at[k, slot],
            device_id=reduce_device(other),
            device_id_type=MESH,
        )

    digit = lax.broadcasted_iota(jnp.int32, (32, TILE), 0)

    def near_tiles(idx_ref, wt_ref, half, first, count):
        def one(step, carry):
            tile = first + step
            lanes = pl.ds(pl.multiple_of(tile * TILE, TILE), TILE)
            out_lanes = pl.ds(pl.multiple_of(half * 512 + tile * TILE, TILE), TILE)
            for k in range(LISTED):
                place = idx_ref[k : k + 1, lanes] - y_hi * LOCAL
                weight = wt_ref[k : k + 1, lanes]
                digit_a[k] = jnp.where(digit == lax.shift_right_arithmetic(place, 5), weight, 0.0)
                digit_b[k] = jnp.where(digit == (place & 31), 1.0, 0.0)
            for group in range(4):
                ones = [digit_b[k, group * 8 : group * 8 + 8, :] for k in range(LISTED)]

                def line(step, carry):
                    for u in range(4):
                        top = step * 4 + u
                        parts = [digit_a[k, pl.ds(top, 1), :] * ones[k] for k in range(LISTED)]
                        while len(parts) > 1:
                            parts = [parts[i] + parts[i + 1] for i in range(0, len(parts), 2)]
                        nmat[pl.ds(pl.multiple_of(top * 32 + group * 8, 8), 8), out_lanes] = parts[0]
                    return carry

                lax.fori_loop(0, 8, line, 0)
            return carry

        lax.fori_loop(0, count, one, 0)

    near_tiles(nidx_ref, nwt_ref, y_hi, 0, EARLY)
    pl.semaphore_wait(barrier, 2 * (GROUP - 1))

    for copy in near_copies():
        copy.start()
    for d in FAR_FIRST:
        pts_copy(d, p).start()
        ag_copy(0, d, q).start()
    ag[0, q] = pkt[0]
    pts[p] = pkt[0]

    near_tiles(nidx_ref, nwt_ref, y_hi, EARLY, 4 - EARLY)
    for copy in near_copies():
        copy.wait_recv()
    near_tiles(far_idx, far_wt, 1 - y_hi, 0, 4)

    lane = lax.broadcasted_iota(jnp.int32, (8, TILE), 1)
    low = lane < PAN
    wide = lax.broadcasted_iota(jnp.int32, (8, 2 * TILE), 1)
    body_lanes = wide < 3 * PAN

    def swap(x):
        return pltpu.roll(x, PAN, 1)

    def join(first, second):
        a, c = first[:, :TILE], first[:, TILE:]
        b, e = second[:, :TILE], second[:, TILE:]
        return (
            jnp.where(low, a, swap(b)),
            jnp.where(low, swap(a), b),
            jnp.where(low, c, swap(e)),
        )

    for d in range(1, GROUP):
        pts_copy(d, (p + d) % GROUP).wait_recv()
    for m in range(GROUP // 2):
        for a, tile in enumerate(join(pts[2 * m], pts[2 * m + 1])):
            tgtb[a, :, m * TILE : (m + 1) * TILE] = jnp.broadcast_to(tile[6:7], (16, TILE))

    def wait_shards(k, rows):
        if rows is None:
            for d in range(1, 4):
                other = own_rows * 4 + (q + d) % 4
                ag_copy(k, d, other).wait_recv()
        else:
            for d in range(4):
                ag_copy(k, d, rows * 4 + d).wait_recv()

    def spread_sources(rows):
        for i in range(4):
            s = rows * 4 + i
            place = pl.ds(pl.multiple_of(s * PAN, PAN), PAN)
            for half in range(2):
                line = ag[0, s, 6:7, half * TILE : (half + 1) * TILE]
                flipped = jnp.transpose(jnp.broadcast_to(line, (TILE, TILE)))
                if half == 0:
                    srcb[0, place] = flipped[:PAN]
                    srcb[1, place] = flipped[PAN:]
                else:
                    srcb[2, place] = flipped[:PAN]
                    srcb[3, place] = flipped[PAN:] * INV_EIGHT_PI

    def build(quarter, chunk):
        def one(step, carry):
            for t in range(CHUNK // TILE):
                rows = pl.ds(pl.multiple_of(quarter * CHUNK + step * 16, 16), 16)
                lanes = pl.ds(pl.multiple_of(chunk * CHUNK + t * TILE, TILE), TILE)
                off = [tgtb[a, :, lanes] - srcb[a, rows, :] for a in range(3)]
                dist = (off[0] * off[0] + off[1] * off[1]) + (off[2] * off[2] + BLOB_SQ)
                inv = lax.rsqrt(dist)
                two = (srcb[3, rows, :] * inv) * (inv * inv)
                near = (dist + BLOB_SQ) * two + nmat[rows, lanes]
                high = near.astype(jnp.bfloat16)
                wts[0, rows, lanes] = high
                wts[1, rows, lanes] = (near - high.astype(jnp.float32)).astype(jnp.bfloat16)
                scaled = [two * v for v in off]
                for a in range(3):
                    wts[2 + a, rows, lanes] = (scaled[a] * off[a]).astype(jnp.bfloat16)
                for a, b, block in MIXED:
                    wts[block, rows, lanes] = (scaled[a] * off[b]).astype(jnp.bfloat16)
            return carry

        lax.fori_loop(0, CHUNK // 16, one, 0)

    def fields(k, rows):
        tiles = [join(ag[k, rows * 4 + 2 * m], ag[k, rows * 4 + 2 * m + 1]) for m in range(2)]
        out = []
        for a in range(3):
            value = jnp.concatenate([tiles[0][a], tiles[1][a]], axis=1)
            high = value.astype(jnp.bfloat16).astype(jnp.float32)
            out.append(jnp.concatenate([high, value - high], axis=0).astype(jnp.bfloat16))
        return out

    def products(field, quarter, chunk):
        rows = pl.ds(pl.multiple_of(quarter * CHUNK, CHUNK), CHUNK)
        lanes = pl.ds(pl.multiple_of(chunk * CHUNK, CHUNK), CHUNK)

        def dot(lhs, block):
            return jnp.dot(lhs, wts[block, rows, lanes], preferred_element_type=jnp.float32)

        stacked = jnp.concatenate(field, axis=0)
        both = dot(stacked, 0) + dot(stacked, 1)
        acc = [both[16 * a : 16 * a + 16] + dot(field[a], 2 + a) for a in range(3)]
        for a, b, block in MIXED:
            both = dot(jnp.concatenate([field[a], field[b]], axis=0), block)
            acc[b] = acc[b] + both[:16]
            acc[a] = acc[a] + both[16:]
        return [v[:8] + v[8:] for v in acc]

    def group_dots(k):
        if k == 0:
            total = jnp.zeros((8, 2 * TILE), jnp.float32)
            for s in range(GROUP):
                total = total + ag[0, s] * ag[0, s]
            return jnp.broadcast_to(jnp.sum(jnp.where(body_lanes, total, 0.0), axis=1, keepdims=True), (8, TILE))
        total = ag[k, 0, :, TILE:]
        for s in range(1, GROUP):
            total = total + ag[k, s, :, TILE:]
        return total

    def apply(k):
        riding = None
        for step, shift in enumerate((0, 1, 3, 2)):
            quarter = (own_rows + shift) % 4
            wait_shards(k, quarter if shift else None)
            if k == 0:
                spread_sources(quarter)
            field = fields(k, quarter)
            if step == 3:
                riding = group_dots(k)
            for turn in (2, 1, 3, 0):
                chunk = (own_lanes + turn) % 4
                if k == 0:
                    build(quarter, chunk)
                sums = products(field, quarter, chunk)
                lanes = pl.ds(pl.multiple_of(chunk * CHUNK, CHUNK), CHUNK)
                if step > 0:
                    sums = [uacc[a, :, lanes] + sums[a] for a in range(3)]
                if step < 3:
                    for a in range(3):
                        uacc[a, :, lanes] = sums[a]
                    continue
                for i in range(4):
                    t, odd = i // 2, i % 2
                    first, second, third = [v[:, t * TILE : (t + 1) * TILE] for v in sums]
                    if odd:
                        first, third = swap(first), swap(third)
                    else:
                        second = swap(second)
                    other = chunk * 4 + i
                    rss[k, other, :, :TILE] = jnp.where(low, first, second)
                    rss[k, other, :, TILE:] = jnp.where(low, third, riding)
                    if turn:
                        rs_copy(k, other, p).start()
                    else:

                        @pl.when(other != p)
                        def _():
                            rs_copy(k, other, p).start()

        return collect(k)

    def collect(k):
        total = rss[k, p]
        for d in range(1, GROUP):
            other = (p + d) % GROUP
            rs_copy(k, other, other).wait_recv()
            total = total + rsr[k, other]
        return total

    def send_packet(k, vector, dots):
        value = jnp.where(body_lanes, vector, 0.0)
        for i, dot in enumerate(dots):
            value = jnp.where(wide == 3 * PAN + i, dot, value)
        pkt[k] = value
        ag[k, q] = value
        for d in FAR_FIRST:
            ag_copy(k, d, q).start()

    def inner(a, b):
        return jnp.sum(jnp.where(body_lanes, a * b, 0.0), axis=1, keepdims=True)

    def pick(total, i):
        return total[:, 3 * PAN + i : 3 * PAN + i + 1]

    def length_of(square, whole):
        return jnp.sqrt(jnp.maximum(square, whole * 1e-7))

    own = jnp.where(body_lanes, pkt[0], 0.0)
    line = jnp.concatenate([self_ref[...], self_ref[...]], axis=1)
    line = jnp.broadcast_to(jnp.concatenate([line, line], axis=1), (8, 2 * TILE))
    self_term = jnp.where(body_lanes, line, 0.0)

    total = apply(0)
    start_norm = jnp.sqrt(pick(total, 0))
    basis0 = own / start_norm
    image0 = (self_term * own + total) / start_norm

    send_packet(1, image0, [inner(basis0, image0), inner(image0, image0)])
    total = apply(1)
    h00 = pick(total, 0)
    square = pick(total, 1)
    h10 = length_of(square - h00 * h00, square)
    basis1 = (image0 - h00 * basis0) / h10
    image1 = (self_term * image0 + total - h00 * image0) / h10

    send_packet(
        2,
        image1,
        [inner(basis1, basis1), inner(basis0, image1), inner(basis1, image1), inner(image1, image1)],
    )
    total = apply(2)
    scale = jnp.sqrt(pick(total, 0))
    second_image = (self_term * image1 + total) / scale
    basis1 = basis1 / scale
    image1 = image1 / scale
    h10 = h10 * scale
    h01 = pick(total, 1) / scale
    h11 = pick(total, 2) / (scale * scale)
    square = pick(total, 3) / (scale * scale)
    h21 = length_of(square - h01 * h01 - h11 * h11, square)
    basis2 = (image1 - h01 * basis0 - h11 * basis1) / h21
    image2 = (second_image - h01 * image0 - h11 * image1) / h21

    send_packet(
        3,
        image2,
        [
            inner(basis2, basis2),
            inner(basis0, image2),
            inner(basis1, image2),
            inner(basis2, image2),
            inner(image2, image2),
        ],
    )
    for d in range(1, GROUP):
        ag_copy(3, d, (q + d) % GROUP).wait_recv()
    riding = group_dots(3)
    for d in range(GROUP):
        rss[3, d, :, TILE:] = riding
    for d in FAR_FIRST:
        rs_copy(3, (p + d) % GROUP, p).start()
    total = collect(3)
    scale = jnp.sqrt(pick(total, 0))
    basis2 = basis2 / scale
    h21 = h21 * scale
    h02 = pick(total, 1) / scale
    h12 = pick(total, 2) / scale
    h22 = pick(total, 3) / (scale * scale)
    square = pick(total, 4) / (scale * scale)
    h32 = jnp.sqrt(jnp.maximum(square - h02 * h02 - h12 * h12 - h22 * h22, 0.0))

    columns = [[h00, h10], [h01, h11, h21], [h02, h12, h22, h32]]
    target = [start_norm] + [jnp.zeros_like(start_norm)] * ITERS
    turns = []
    for k in range(ITERS):
        column = columns[k]
        for j in range(k):
            cosine, sine = turns[j]
            column[j], column[j + 1] = (
                cosine * column[j] + sine * column[j + 1],
                cosine * column[j + 1] - sine * column[j],
            )
        radius = jnp.sqrt(column[k] * column[k] + column[k + 1] * column[k + 1])
        cosine, sine = column[k] / radius, column[k + 1] / radius
        turns.append((cosine, sine))
        column[k] = radius
        target[k + 1] = -sine * target[k]
        target[k] = cosine * target[k]
    coeffs = [None] * ITERS
    for k in range(ITERS - 1, -1, -1):
        accum = target[k]
        for i in range(k + 1, ITERS):
            accum = accum - columns[i][k] * coeffs[i]
        coeffs[k] = accum / columns[k][k]
    density = coeffs[0] * basis0 + coeffs[1] * basis1 + coeffs[2] * basis2
    out_ref[:, 0, :] = density[:6, :PAN]
    out_ref[:, 1, :] = density[:6, PAN : 2 * PAN]
    out_ref[:, 2, :] = density[:6, 2 * PAN : 3 * PAN]

    for copy in near_copies():
        copy.wait_send()
    for d in range(1, GROUP):
        pts_copy(d, p).wait_send()
        for k in range(ROUNDS):
            ag_copy(k, d, q).wait_send()
            rs_copy(k, (p + d) % GROUP, p).wait_send()


def body(velocity, points, panel_area, self_term, near_index, near_weight):
    vmem = pl.BlockSpec(memory_space=pltpu.VMEM)
    rhs = velocity.shape[0]
    return pl.pallas_call(
        kernel,
        out_shape=jax.ShapeDtypeStruct((rhs, 3, PAN), jnp.float32),
        in_specs=[vmem] * 6,
        out_specs=vmem,
        scratch_shapes=[
            pltpu.VMEM((ROUNDS, 8, 4 * PAN), jnp.float32),
            pltpu.VMEM((ROUNDS, GROUP, 8, 4 * PAN), jnp.float32),
            pltpu.VMEM((GROUP, 8, 4 * PAN), jnp.float32),
            pltpu.VMEM((ROUNDS, GROUP, 8, 4 * PAN), jnp.float32),
            pltpu.VMEM((ROUNDS, GROUP, 8, 4 * PAN), jnp.float32),
            pltpu.VMEM((LISTED, 512), jnp.int32),
            pltpu.VMEM((LISTED, 512), jnp.float32),
            pltpu.VMEM((LISTED, 32, TILE), jnp.float32),
            pltpu.VMEM((LISTED, 32, TILE), jnp.float32),
            pltpu.VMEM((4, LOCAL, TILE), jnp.float32),
            pltpu.VMEM((3, 16, LOCAL), jnp.float32),
            pltpu.VMEM((LOCAL, LOCAL), jnp.float32),
            pltpu.VMEM((BLOCKS, LOCAL, LOCAL), jnp.bfloat16),
            pltpu.VMEM((3, 8, LOCAL), jnp.float32),
            pltpu.SemaphoreType.DMA((ROUNDS, GROUP)),
            pltpu.SemaphoreType.DMA((ROUNDS, GROUP)),
            pltpu.SemaphoreType.DMA((GROUP,)),
            pltpu.SemaphoreType.DMA((GROUP,)),
            pltpu.SemaphoreType.DMA((ROUNDS, GROUP)),
            pltpu.SemaphoreType.DMA((ROUNDS, GROUP)),
            pltpu.SemaphoreType.DMA((2,)),
            pltpu.SemaphoreType.DMA((2,)),
        ],
        compiler_params=pltpu.CompilerParams(
            collective_id=0, has_side_effects=True, vmem_limit_bytes=56 * 1024 * 1024
        ),
    )(
        velocity,
        points,
        panel_area.reshape(1, PAN),
        self_term.reshape(1, PAN),
        near_index.T,
        near_weight.T,
    )


def solution(mesh):
    return jax.shard_map(
        body,
        mesh=mesh,
        in_specs=(
            P(None, None, ("row", "col")),
            P(None, ("row", "col")),
            P(("row", "col")),
            P(("row", "col")),
            P("row", "col"),
            P("row", "col"),
        ),
        out_specs=P(None, None, ("row", "col")),
        check_vma=False,
    )
```

time: 89.1 us -> 80.6 us (0.905)
  local copies, waits for them, and re-layouts: 4.58 us -> 1.31 us
  Pallas kernels: 82 us -> 79.1 us
  other arithmetic: 2.21 us -> 0 us
    reshape x3 -> x0, local copies, waits for them, and re-layouts: 2.93 us -> none  [the longest x1 1.37 us: body(): return result[:rhs, :3 * PAN].reshape(rhs, 3, PAN)]
    pallas_call x1, Pallas kernels: 82 us -> 79.1 us  [body(): pl.pallas_call(kernel, out_shape=jax.ShapeDtypeStruct((rhs, 3, PAN), jnp....]
    concatenate x2 -> x0, other arithmetic: 2.21 us -> none  [the longest x1 1.33 us: body(): packet = jnp.concatenate([top, places, own], axis=0)]
where the time goes in v2:
time: 80.6 us; the launch traced here: 80.4 us
  Pallas kernels  79.1 us (98%)
  local copies, waits for them, and re-layouts  1.31 us (2%)
    pallas_call x1, Pallas kernels, body(): pl.pallas_call(kernel, out_shape=jax.ShapeDtypeStruct((rhs, 3, PAN), jnp....  79.1 us

profile of v2, /device:TPU:1, one launch (start us, length us, event | category | flops | bytes accessed | tf_op | source)
XLA Modules:
  0.0 80.4 jit_solution(1848158566599971109)
XLA Ops:
  0.0 79.1 %shard_map.64 = f32[6,3,64]{2,1,0:T(4,128)} custom-call(f32[6,3,64]{2,1,0:T(4,128)} %vel_ref.1, f32[3,64]{1,0:T(4,128)} %points_ref.1, f32[1,64]{1,0:T(1,128)} %bitcast.6, f32[1,64]{1,0:T(1,128)} %bitcast.7, s32[16,512]{1,0:T(8,128)} %bitcast.4, f32[16,512]{1,0:T(8,128)} %bitcast.5), custom_call_target="tpu_custom_call" | custom-call | tf_op jit(solution)/shard_map/pallas_call | solution.py:453
  79.1 1.3 %copy.8 = f32[6,3,64]{2,1,0:T(4,128)} copy(f32[6,3,64]{2,1,0:T(4,128)} %shard_map.64) | data formatting | bytes 9216

commit v3 on v2

--- a/solution.py
+++ b/solution.py
@@ -1,4 +1,3 @@
-import functools
 import math
 
 import jax
@@ -26,13 +25,19 @@
 
 
 def kernel(
+    vel_hbm,
+    points_hbm,
+    area_hbm,
+    self_hbm,
+    nidx_hbm,
+    nwt_hbm,
+    out_ref,
     vel_ref,
     points_ref,
     area_ref,
     self_ref,
     nidx_ref,
     nwt_ref,
-    out_ref,
     pkt,
     ag,
     pts,
@@ -55,6 +60,7 @@
     rs_recv,
     near_send,
     near_recv,
+    load_sem,
 ):
     row = lax.axis_index("row")
     col = lax.axis_index("col")
@@ -74,6 +80,24 @@
     for d in range(1, GROUP):
         pl.semaphore_signal(barrier, inc=1, device_id=gather_device((q + d) % GROUP), device_id_type=MESH)
         pl.semaphore_signal(barrier, inc=1, device_id=reduce_device((p + d) % GROUP), device_id_type=MESH)
+
+    loads = [
+        pltpu.make_async_copy(outer, inner, load_sem.at[i])
+        for i, (outer, inner) in enumerate(
+            (
+                (nidx_hbm, nidx_ref),
+                (nwt_hbm, nwt_ref),
+                (vel_hbm, vel_ref),
+                (points_hbm, points_ref),
+                (area_hbm, area_ref),
+                (self_hbm, self_ref),
+            )
+        )
+    ]
+    for load in loads:
+        load.start()
+    for load in loads:
+        load.wait()
 
     pkt[0] = jnp.zeros((8, 2 * TILE), jnp.float32)
     pkt[0, :6, :TILE] = jnp.concatenate([vel_ref[:, 0, :], vel_ref[:, 1, :]], axis=1)
@@ -103,8 +127,8 @@
         return pltpu.make_async_remote_copy(
             src_ref=window(pkt.at[k], k),
             dst_ref=window(ag.at[k, slot], k),
-            send_sem=ag_send.at[k, d],
-            recv_sem=ag_recv.at[k, slot],
+            send_sem=ag_send.at[k],
+            recv_sem=ag_recv.at[k, own_rows],
             device_id=gather_device((q + d) % GROUP),
             device_id_type=MESH,
         )
@@ -113,8 +137,8 @@
         return pltpu.make_async_remote_copy(
             src_ref=pkt.at[0],
             dst_ref=pts.at[slot],
-            send_sem=pts_send.at[d],
-            recv_sem=pts_recv.at[slot],
+            send_sem=pts_send.at[0],
+            recv_sem=pts_recv.at[0],
             device_id=reduce_device((p + d) % GROUP),
             device_id_type=MESH,
         )
@@ -123,11 +147,26 @@
         return pltpu.make_async_remote_copy(
             src_ref=window(rss.at[k, other], k),
             dst_ref=window(rsr.at[k, slot], k),
-            send_sem=rs_send.at[k, other],
-            recv_sem=rs_recv.at[k, slot],
+            send_sem=rs_send.at[k],
+            recv_sem=rs_recv.at[k],
             device_id=reduce_device(other),
             device_id_type=MESH,
         )
+
+    def whole(ref, send, recv):
+        return pltpu.make_async_remote_copy(
+            src_ref=ref,
+            dst_ref=ref,
+            send_sem=send,
+            recv_sem=recv,
+            device_id=partner,
+            device_id_type=MESH,
+        )
+
+    def several(ref, k, first, count):
+        if k < ITERS:
+            return ref.at[k, pl.ds(first, count)]
+        return ref.at[k, pl.ds(first, count), :, pl.ds(TILE, TILE)]
 
     digit = lax.broadcasted_iota(jnp.int32, (32, TILE), 0)
 
@@ -135,7 +174,6 @@
         def one(step, carry):
             tile = first + step
             lanes = pl.ds(pl.multiple_of(tile * TILE, TILE), TILE)
-            out_lanes = pl.ds(pl.multiple_of(half * 512 + tile * TILE, TILE), TILE)
             for k in range(LISTED):
                 place = idx_ref[k : k + 1, lanes] - y_hi * LOCAL
                 weight = wt_ref[k : k + 1, lanes]
@@ -145,15 +183,15 @@
                 ones = [digit_b[k, group * 8 : group * 8 + 8, :] for k in range(LISTED)]
 
                 def line(step, carry):
-                    for u in range(4):
-                        top = step * 4 + u
+                    for u in range(8):
+                        top = step * 8 + u
                         parts = [digit_a[k, pl.ds(top, 1), :] * ones[k] for k in range(LISTED)]
                         while len(parts) > 1:
                             parts = [parts[i] + parts[i + 1] for i in range(0, len(parts), 2)]
-                        nmat[pl.ds(pl.multiple_of(top * 32 + group * 8, 8), 8), out_lanes] = parts[0]
+                        nmat[half * 4 + tile, pl.ds(pl.multiple_of(top * 32 + group * 8, 8), 8), :] = parts[0]
                     return carry
 
-                lax.fori_loop(0, 8, line, 0)
+                lax.fori_loop(0, 4, line, 0)
             return carry
 
         lax.fori_loop(0, count, one, 0)
@@ -191,20 +229,15 @@
             jnp.where(low, c, swap(e)),
         )
 
-    for d in range(1, GROUP):
-        pts_copy(d, (p + d) % GROUP).wait_recv()
+    whole(pts.at[pl.ds(0, GROUP - 1)], pts_send.at[0], pts_recv.at[0]).wait_recv()
     for m in range(GROUP // 2):
         for a, tile in enumerate(join(pts[2 * m], pts[2 * m + 1])):
             tgtb[a, :, m * TILE : (m + 1) * TILE] = jnp.broadcast_to(tile[6:7], (16, TILE))
 
     def wait_shards(k, rows):
-        if rows is None:
-            for d in range(1, 4):
-                other = own_rows * 4 + (q + d) % 4
-                ag_copy(k, d, other).wait_recv()
-        else:
-            for d in range(4):
-                ag_copy(k, d, rows * 4 + d).wait_recv()
+        count = 3 if rows is None else 4
+        rows = own_rows if rows is None else rows
+        whole(several(ag, k, rows * 4, count), ag_send.at[k], ag_recv.at[k, rows]).wait_recv()
 
     def spread_sources(rows):
         for i in range(4):
@@ -222,25 +255,26 @@
 
     def build(quarter, chunk):
         def one(step, carry):
-            for t in range(CHUNK // TILE):
-                rows = pl.ds(pl.multiple_of(quarter * CHUNK + step * 16, 16), 16)
+            for h, t in ((0, 0), (0, 1), (1, 0), (1, 1)):
+                rows = pl.ds(pl.multiple_of(quarter * CHUNK + step * 32 + h * 16, 16), 16)
+                part = slice(t * TILE, (t + 1) * TILE)
                 lanes = pl.ds(pl.multiple_of(chunk * CHUNK + t * TILE, TILE), TILE)
                 off = [tgtb[a, :, lanes] - srcb[a, rows, :] for a in range(3)]
                 dist = (off[0] * off[0] + off[1] * off[1]) + (off[2] * off[2] + BLOB_SQ)
                 inv = lax.rsqrt(dist)
                 two = (srcb[3, rows, :] * inv) * (inv * inv)
-                near = (dist + BLOB_SQ) * two + nmat[rows, lanes]
+                near = (dist + BLOB_SQ) * two + nmat[chunk * 2 + t, rows, :]
                 high = near.astype(jnp.bfloat16)
-                wts[0, rows, lanes] = high
-                wts[1, rows, lanes] = (near - high.astype(jnp.float32)).astype(jnp.bfloat16)
+                wts[0, chunk, rows, part] = high
+                wts[1, chunk, rows, part] = (near - high.astype(jnp.float32)).astype(jnp.bfloat16)
                 scaled = [two * v for v in off]
                 for a in range(3):
-                    wts[2 + a, rows, lanes] = (scaled[a] * off[a]).astype(jnp.bfloat16)
+                    wts[2 + a, chunk, rows, part] = (scaled[a] * off[a]).astype(jnp.bfloat16)
                 for a, b, block in MIXED:
-                    wts[block, rows, lanes] = (scaled[a] * off[b]).astype(jnp.bfloat16)
+                    wts[block, chunk, rows, part] = (scaled[a] * off[b]).astype(jnp.bfloat16)
             return carry
 
-        lax.fori_loop(0, CHUNK // 16, one, 0)
+        lax.fori_loop(0, CHUNK // 32, one, 0)
 
     def fields(k, rows):
         tiles = [join(ag[k, rows * 4 + 2 * m], ag[k, rows * 4 + 2 * m + 1]) for m in range(2)]
@@ -253,10 +287,9 @@
 
     def products(field, quarter, chunk):
         rows = pl.ds(pl.multiple_of(quarter * CHUNK, CHUNK), CHUNK)
-        lanes = pl.ds(pl.multiple_of(chunk * CHUNK, CHUNK), CHUNK)
 
         def dot(lhs, block):
-            return jnp.dot(lhs, wts[block, rows, lanes], preferred_element_type=jnp.float32)
+            return jnp.dot(lhs, wts[block, chunk, rows, :], preferred_element_type=jnp.float32)
 
         stacked = jnp.concatenate(field, axis=0)
         both = dot(stacked, 0) + dot(stacked, 1)
@@ -278,6 +311,27 @@
             total = total + ag[k, s, :, TILE:]
         return total
 
+    def send_sums(k, turn, chunk, sums, riding):
+        for i in range(4):
+            t, odd = i // 2, i % 2
+            first, second, third = [v[:, t * TILE : (t + 1) * TILE] for v in sums]
+            if odd:
+                first, third = swap(first), swap(third)
+            else:
+                second = swap(second)
+            other = chunk * 4 + i
+            rss[k, other, :, :TILE] = jnp.where(low, first, second)
+            rss[k, other, :, TILE:] = jnp.where(low, third, riding)
+        for i in range(4):
+            other = chunk * 4 + i
+            if turn:
+                rs_copy(k, other, p).start()
+            else:
+
+                @pl.when(other != p)
+                def _():
+                    rs_copy(k, other, p).start()
+
     def apply(k):
         riding = None
         for step, shift in enumerate((0, 1, 3, 2)):
@@ -288,45 +342,29 @@
             field = fields(k, quarter)
             if step == 3:
                 riding = group_dots(k)
-            for turn in (2, 1, 3, 0):
-                chunk = (own_lanes + turn) % 4
+            for turns in ((2, 1), (3, 0)):
+                chunks = [(own_lanes + turn) % 4 for turn in turns]
                 if k == 0:
-                    build(quarter, chunk)
-                sums = products(field, quarter, chunk)
-                lanes = pl.ds(pl.multiple_of(chunk * CHUNK, CHUNK), CHUNK)
-                if step > 0:
-                    sums = [uacc[a, :, lanes] + sums[a] for a in range(3)]
-                if step < 3:
-                    for a in range(3):
-                        uacc[a, :, lanes] = sums[a]
-                    continue
-                for i in range(4):
-                    t, odd = i // 2, i % 2
-                    first, second, third = [v[:, t * TILE : (t + 1) * TILE] for v in sums]
-                    if odd:
-                        first, third = swap(first), swap(third)
+                    for chunk in chunks:
+                        build(quarter, chunk)
+                results = [products(field, quarter, chunk) for chunk in chunks]
+                for turn, chunk, sums in zip(turns, chunks, results):
+                    lanes = pl.ds(pl.multiple_of(chunk * CHUNK, CHUNK), CHUNK)
+                    if step > 0:
+                        sums = [uacc[a, :, lanes] + sums[a] for a in range(3)]
+                    if step < 3:
+                        for a in range(3):
+                            uacc[a, :, lanes] = sums[a]
                     else:
-                        second = swap(second)
-                    other = chunk * 4 + i
-                    rss[k, other, :, :TILE] = jnp.where(low, first, second)
-                    rss[k, other, :, TILE:] = jnp.where(low, third, riding)
-                    if turn:
-                        rs_copy(k, other, p).start()
-                    else:
-
-                        @pl.when(other != p)
-                        def _():
-                            rs_copy(k, other, p).start()
-
+                        send_sums(k, turn, chunk, sums, riding)
         return collect(k)
 
     def collect(k):
-        total = rss[k, p]
-        for d in range(1, GROUP):
-            other = (p + d) % GROUP
-            rs_copy(k, other, other).wait_recv()
-            total = total + rsr[k, other]
-        return total
+        whole(several(rsr, k, 0, GROUP - 1), rs_send.at[k], rs_recv.at[k]).wait_recv()
+        parts = [rss[k, p]] + [rsr[k, (p + d) % GROUP] for d in range(1, GROUP)]
+        while len(parts) > 1:
+            parts = [parts[i] + parts[i + 1] for i in range(0, len(parts), 2)]
+        return parts[0]
 
     def send_packet(k, vector, dots):
         value = jnp.where(body_lanes, vector, 0.0)
@@ -393,8 +431,8 @@
             inner(image2, image2),
         ],
     )
-    for d in range(1, GROUP):
-        ag_copy(3, d, (q + d) % GROUP).wait_recv()
+    for shift in range(4):
+        wait_shards(3, (own_rows + shift) % 4 if shift else None)
     riding = group_dots(3)
     for d in range(GROUP):
         rss[3, d, :, TILE:] = riding
@@ -440,11 +478,10 @@
 
     for copy in near_copies():
         copy.wait_send()
-    for d in range(1, GROUP):
-        pts_copy(d, p).wait_send()
-        for k in range(ROUNDS):
-            ag_copy(k, d, q).wait_send()
-            rs_copy(k, (p + d) % GROUP, p).wait_send()
+    whole(rss.at[0, pl.ds(0, GROUP - 1)], pts_send.at[0], pts_recv.at[0]).wait_send()
+    for k in range(ROUNDS):
+        whole(several(rss, k, 0, GROUP - 1), ag_send.at[k], ag_recv.at[k, 0]).wait_send()
+        whole(several(rss, k, 0, GROUP - 1), rs_send.at[k], rs_recv.at[k]).wait_send()
 
 
 def body(velocity, points, panel_area, self_term, near_index, near_weight):
@@ -453,9 +490,15 @@
     return pl.pallas_call(
         kernel,
         out_shape=jax.ShapeDtypeStruct((rhs, 3, PAN), jnp.float32),
-        in_specs=[vmem] * 6,
+        in_specs=[pl.BlockSpec(memory_space=pl.ANY)] * 6,
         out_specs=vmem,
         scratch_shapes=[
+            pltpu.VMEM((rhs, 3, PAN), jnp.float32),
+            pltpu.VMEM((3, PAN), jnp.float32),
+            pltpu.VMEM((1, PAN), jnp.float32),
+            pltpu.VMEM((1, PAN), jnp.float32),
+            pltpu.VMEM((LISTED, 512), jnp.int32),
+            pltpu.VMEM((LISTED, 512), jnp.float32),
             pltpu.VMEM((ROUNDS, 8, 4 * PAN), jnp.float32),
             pltpu.VMEM((ROUNDS, GROUP, 8, 4 * PAN), jnp.float32),
             pltpu.VMEM((GROUP, 8, 4 * PAN), jnp.float32),
@@ -467,17 +510,18 @@
             pltpu.VMEM((LISTED, 32, TILE), jnp.float32),
             pltpu.VMEM((4, LOCAL, TILE), jnp.float32),
             pltpu.VMEM((3, 16, LOCAL), jnp.float32),
-            pltpu.VMEM((LOCAL, LOCAL), jnp.float32),
-            pltpu.VMEM((BLOCKS, LOCAL, LOCAL), jnp.bfloat16),
+            pltpu.VMEM((8, LOCAL, TILE), jnp.float32),
+            pltpu.VMEM((BLOCKS, 4, LOCAL, CHUNK), jnp.bfloat16),
             pltpu.VMEM((3, 8, LOCAL), jnp.float32),
-            pltpu.SemaphoreType.DMA((ROUNDS, GROUP)),
-            pltpu.SemaphoreType.DMA((ROUNDS, GROUP)),
-            pltpu.SemaphoreType.DMA((GROUP,)),
-            pltpu.SemaphoreType.DMA((GROUP,)),
-            pltpu.SemaphoreType.DMA((ROUNDS, GROUP)),
-            pltpu.SemaphoreType.DMA((ROUNDS, GROUP)),
+            pltpu.SemaphoreType.DMA((ROUNDS,)),
+            pltpu.SemaphoreType.DMA((ROUNDS, 4)),
+            pltpu.SemaphoreType.DMA((1,)),
+            pltpu.SemaphoreType.DMA((1,)),
+            pltpu.SemaphoreType.DMA((ROUNDS,)),
+            pltpu.SemaphoreType.DMA((ROUNDS,)),
             pltpu.SemaphoreType.DMA((2,)),
             pltpu.SemaphoreType.DMA((2,)),
+            pltpu.SemaphoreType.DMA((6,)),
         ],
         compiler_params=pltpu.CompilerParams(
             collective_id=0, has_side_effects=True, vmem_limit_bytes=56 * 1024 * 1024

time: 80.6 us -> 70.9 us (0.88)
  Pallas kernels: 79.1 us -> 69.4 us
    pallas_call x1, Pallas kernels: 79.1 us -> 69.4 us  [body(): pl.pallas_call(kernel, out_shape=jax.ShapeDtypeStruct((rhs, 3, PAN), jnp....]
where the time goes in v3:
time: 70.9 us; the launch traced here: 70.7 us
  Pallas kernels  69.4 us (98%)
  local copies, waits for them, and re-layouts  1.31 us (2%)
    pallas_call x1, Pallas kernels, body(): pl.pallas_call(kernel, out_shape=jax.ShapeDtypeStruct((rhs, 3, PAN), jnp....  69.4 us

profile of v3, /device:TPU:1, one launch (start us, length us, event | category | flops | bytes accessed | tf_op | source)
XLA Modules:
  0.0 70.7 jit_solution(5662597223293053467)
XLA Ops:
  0.0 69.4 %shard_map.64 = f32[6,3,64]{2,1,0:T(4,128)} custom-call(f32[6,3,64]{2,1,0:T(4,128)} %vel_hbm.1, f32[3,64]{1,0:T(4,128)} %points_hbm.1, f32[1,64]{1,0:T(1,128)} %bitcast.6, f32[1,64]{1,0:T(1,128)} %bitcast.7, s32[16,512]{1,0:T(8,128)} %bitcast.4, f32[16,512]{1,0:T(8,128)} %bitcast.5), custom_call_target="tpu_custom_call" | custom-call | tf_op jit(solution)/shard_map/pallas_call | solution.py:490
  69.4 1.3 %copy.8 = f32[6,3,64]{2,1,0:T(4,128)} copy(f32[6,3,64]{2,1,0:T(4,128)} %shard_map.64) | data formatting | bytes 9216

commit v4 on v3

--- a/solution.py
+++ b/solution.py
@@ -19,9 +19,12 @@
 BLOCKS = 8
 FAR_FIRST = (8, 9, 7, 6, 10, 5, 11, 4, 12, 3, 13, 2, 14, 1, 15)
 CHUNK = 256
+HALF = 512
+PAD = 16
+ROWS = 6
 TILE = 128
 ROUNDS = ITERS + 1
-EARLY = 3
+EARLY = 4
 
 
 def kernel(
@@ -68,7 +71,6 @@
     q = row % GROUP
     p = y_hi * 8 + col
     own_rows = q // 4
-    own_lanes = p // 4
 
     def gather_device(other):
         return (y_hi * GROUP + other, col)
@@ -99,11 +101,10 @@
     for load in loads:
         load.wait()
 
+    spare = [points_ref[0:1], points_ref[1:2], points_ref[2:3], area_ref[...], jnp.zeros((2, PAN), jnp.float32)]
     pkt[0] = jnp.zeros((8, 2 * TILE), jnp.float32)
-    pkt[0, :6, :TILE] = jnp.concatenate([vel_ref[:, 0, :], vel_ref[:, 1, :]], axis=1)
-    pkt[0, :6, TILE:] = jnp.concatenate([vel_ref[:, 2, :], jnp.zeros((6, PAN), jnp.float32)], axis=1)
-    pkt[0, 6:7, :TILE] = jnp.concatenate([points_ref[0:1], points_ref[1:2]], axis=1)
-    pkt[0, 6:7, TILE:] = jnp.concatenate([points_ref[2:3], area_ref[...]], axis=1)
+    pkt[0, :ROWS, :TILE] = jnp.concatenate([vel_ref[:, 0, :], vel_ref[:, 1, :]], axis=1)
+    pkt[0, :ROWS, TILE:] = jnp.concatenate([vel_ref[:, 2, :], jnp.concatenate(spare, axis=0)], axis=1)
 
     partner = ((1 - y_hi) * GROUP + q, col)
 
@@ -121,7 +122,7 @@
         ]
 
     def window(ref, k):
-        return ref if k < ITERS else ref.at[:, pl.ds(TILE, TILE)]
+        return ref.at[pl.ds(0, ROWS)] if k < ITERS else ref.at[pl.ds(0, ROWS), pl.ds(TILE, TILE)]
 
     def ag_copy(k, d, slot):
         return pltpu.make_async_remote_copy(
@@ -135,8 +136,8 @@
 
     def pts_copy(d, slot):
         return pltpu.make_async_remote_copy(
-            src_ref=pkt.at[0],
-            dst_ref=pts.at[slot],
+            src_ref=window(pkt.at[0], 0),
+            dst_ref=window(pts.at[slot], 0),
             send_sem=pts_send.at[0],
             recv_sem=pts_recv.at[0],
             device_id=reduce_device((p + d) % GROUP),
@@ -165,8 +166,8 @@
 
     def several(ref, k, first, count):
         if k < ITERS:
-            return ref.at[k, pl.ds(first, count)]
-        return ref.at[k, pl.ds(first, count), :, pl.ds(TILE, TILE)]
+            return ref.at[k, pl.ds(first, count), pl.ds(0, ROWS)]
+        return ref.at[k, pl.ds(first, count), pl.ds(0, ROWS), pl.ds(TILE, TILE)]
 
     digit = lax.broadcasted_iota(jnp.int32, (32, TILE), 0)
 
@@ -229,10 +230,11 @@
             jnp.where(low, c, swap(e)),
         )
 
-    whole(pts.at[pl.ds(0, GROUP - 1)], pts_send.at[0], pts_recv.at[0]).wait_recv()
+    whole(pts.at[pl.ds(0, GROUP - 1), pl.ds(0, ROWS)], pts_send.at[0], pts_recv.at[0]).wait_recv()
     for m in range(GROUP // 2):
-        for a, tile in enumerate(join(pts[2 * m], pts[2 * m + 1])):
-            tgtb[a, :, m * TILE : (m + 1) * TILE] = jnp.broadcast_to(tile[6:7], (16, TILE))
+        tile = jnp.where(low, swap(pts[2 * m, :, TILE:]), pts[2 * m + 1, :, TILE:])
+        for a in range(3):
+            tgtb[a, :, m * TILE : (m + 1) * TILE] = jnp.broadcast_to(tile[a : a + 1], (16, TILE))
 
     def wait_shards(k, rows):
         count = 3 if rows is None else 4
@@ -243,38 +245,37 @@
         for i in range(4):
             s = rows * 4 + i
             place = pl.ds(pl.multiple_of(s * PAN, PAN), PAN)
-            for half in range(2):
-                line = ag[0, s, 6:7, half * TILE : (half + 1) * TILE]
+            tile = ag[0, s, :, TILE:]
+            moved = swap(tile)
+            for pair in range(2):
+                line = jnp.where(low[:1], moved[2 * pair : 2 * pair + 1], tile[2 * pair + 1 : 2 * pair + 2])
                 flipped = jnp.transpose(jnp.broadcast_to(line, (TILE, TILE)))
-                if half == 0:
-                    srcb[0, place] = flipped[:PAN]
-                    srcb[1, place] = flipped[PAN:]
-                else:
-                    srcb[2, place] = flipped[:PAN]
-                    srcb[3, place] = flipped[PAN:] * INV_EIGHT_PI
-
-    def build(quarter, chunk):
+                srcb[2 * pair, place] = flipped[:PAN]
+                srcb[2 * pair + 1, place] = flipped[PAN:] if pair == 0 else flipped[PAN:] * INV_EIGHT_PI
+
+    def build(quarter, half):
         def one(step, carry):
-            for h, t in ((0, 0), (0, 1), (1, 0), (1, 1)):
-                rows = pl.ds(pl.multiple_of(quarter * CHUNK + step * 32 + h * 16, 16), 16)
-                part = slice(t * TILE, (t + 1) * TILE)
-                lanes = pl.ds(pl.multiple_of(chunk * CHUNK + t * TILE, TILE), TILE)
-                off = [tgtb[a, :, lanes] - srcb[a, rows, :] for a in range(3)]
+            rows = pl.ds(pl.multiple_of(quarter * CHUNK + step * 16, 16), 16)
+            source = [srcb[i, rows, :] for i in range(4)]
+            for t in range(HALF // TILE):
+                tile = half * (HALF // TILE) + t
+                lanes = pl.ds(pl.multiple_of(tile * TILE, TILE), TILE)
+                off = [tgtb[a, :, lanes] - source[a] for a in range(3)]
                 dist = (off[0] * off[0] + off[1] * off[1]) + (off[2] * off[2] + BLOB_SQ)
                 inv = lax.rsqrt(dist)
-                two = (srcb[3, rows, :] * inv) * (inv * inv)
-                near = (dist + BLOB_SQ) * two + nmat[chunk * 2 + t, rows, :]
+                two = (source[3] * inv) * (inv * inv)
+                near = (dist + BLOB_SQ) * two + nmat[tile, rows, :]
                 high = near.astype(jnp.bfloat16)
-                wts[0, chunk, rows, part] = high
-                wts[1, chunk, rows, part] = (near - high.astype(jnp.float32)).astype(jnp.bfloat16)
+                wts[0, tile, rows, :] = high
+                wts[1, tile, rows, :] = (near - high.astype(jnp.float32)).astype(jnp.bfloat16)
                 scaled = [two * v for v in off]
                 for a in range(3):
-                    wts[2 + a, chunk, rows, part] = (scaled[a] * off[a]).astype(jnp.bfloat16)
+                    wts[2 + a, tile, rows, :] = (scaled[a] * off[a]).astype(jnp.bfloat16)
                 for a, b, block in MIXED:
-                    wts[block, chunk, rows, part] = (scaled[a] * off[b]).astype(jnp.bfloat16)
+                    wts[block, tile, rows, :] = (scaled[a] * off[b]).astype(jnp.bfloat16)
             return carry
 
-        lax.fori_loop(0, CHUNK // 32, one, 0)
+        lax.fori_loop(0, CHUNK // 16, one, 0)
 
     def fields(k, rows):
         tiles = [join(ag[k, rows * 4 + 2 * m], ag[k, rows * 4 + 2 * m + 1]) for m in range(2)]
@@ -285,11 +286,12 @@
             out.append(jnp.concatenate([high, value - high], axis=0).astype(jnp.bfloat16))
         return out
 
-    def products(field, quarter, chunk):
+    def products(field, quarter, half):
         rows = pl.ds(pl.multiple_of(quarter * CHUNK, CHUNK), CHUNK)
 
         def dot(lhs, block):
-            return jnp.dot(lhs, wts[block, chunk, rows, :], preferred_element_type=jnp.float32)
+            tiles = [wts[block, half * (HALF // TILE) + t, rows, :] for t in range(HALF // TILE)]
+            return jnp.dot(lhs, jnp.concatenate(tiles, axis=1), preferred_element_type=jnp.float32)
 
         stacked = jnp.concatenate(field, axis=0)
         both = dot(stacked, 0) + dot(stacked, 1)
@@ -311,26 +313,27 @@
             total = total + ag[k, s, :, TILE:]
         return total
 
-    def send_sums(k, turn, chunk, sums, riding):
-        for i in range(4):
+    def send_sums(k, half, near, sums, riding):
+        for i in range(8):
             t, odd = i // 2, i % 2
             first, second, third = [v[:, t * TILE : (t + 1) * TILE] for v in sums]
             if odd:
                 first, third = swap(first), swap(third)
             else:
                 second = swap(second)
-            other = chunk * 4 + i
+            other = half * 8 + i
             rss[k, other, :, :TILE] = jnp.where(low, first, second)
             rss[k, other, :, TILE:] = jnp.where(low, third, riding)
-        for i in range(4):
-            other = chunk * 4 + i
-            if turn:
-                rs_copy(k, other, p).start()
-            else:
+        for i in range(8):
+            other = half * 8 + i
+            if near:
 
                 @pl.when(other != p)
                 def _():
                     rs_copy(k, other, p).start()
+
+            else:
+                rs_copy(k, other, p).start()
 
     def apply(k):
         riding = None
@@ -342,21 +345,19 @@
             field = fields(k, quarter)
             if step == 3:
                 riding = group_dots(k)
-            for turns in ((2, 1), (3, 0)):
-                chunks = [(own_lanes + turn) % 4 for turn in turns]
+            for near in range(2):
+                half = y_hi if near else 1 - y_hi
                 if k == 0:
-                    for chunk in chunks:
-                        build(quarter, chunk)
-                results = [products(field, quarter, chunk) for chunk in chunks]
-                for turn, chunk, sums in zip(turns, chunks, results):
-                    lanes = pl.ds(pl.multiple_of(chunk * CHUNK, CHUNK), CHUNK)
-                    if step > 0:
-                        sums = [uacc[a, :, lanes] + sums[a] for a in range(3)]
-                    if step < 3:
-                        for a in range(3):
-                            uacc[a, :, lanes] = sums[a]
-                    else:
-                        send_sums(k, turn, chunk, sums, riding)
+                    build(quarter, half)
+                sums = products(field, quarter, half)
+                lanes = pl.ds(pl.multiple_of(half * HALF, HALF), HALF)
+                if step > 0:
+                    sums = [uacc[a, :, lanes] + sums[a] for a in range(3)]
+                if step < 3:
+                    for a in range(3):
+                        uacc[a, :, lanes] = sums[a]
+                else:
+                    send_sums(k, half, near, sums, riding)
         return collect(k)
 
     def collect(k):
@@ -478,7 +479,7 @@
 
     for copy in near_copies():
         copy.wait_send()
-    whole(rss.at[0, pl.ds(0, GROUP - 1)], pts_send.at[0], pts_recv.at[0]).wait_send()
+    whole(several(rss, 0, 0, GROUP - 1), pts_send.at[0], pts_recv.at[0]).wait_send()
     for k in range(ROUNDS):
         whole(several(rss, k, 0, GROUP - 1), ag_send.at[k], ag_recv.at[k, 0]).wait_send()
         whole(several(rss, k, 0, GROUP - 1), rs_send.at[k], rs_recv.at[k]).wait_send()
@@ -511,7 +512,7 @@
             pltpu.VMEM((4, LOCAL, TILE), jnp.float32),
             pltpu.VMEM((3, 16, LOCAL), jnp.float32),
             pltpu.VMEM((8, LOCAL, TILE), jnp.float32),
-            pltpu.VMEM((BLOCKS, 4, LOCAL, CHUNK), jnp.bfloat16),
+            pltpu.VMEM((BLOCKS, 8, LOCAL + PAD, TILE), jnp.bfloat16),
             pltpu.VMEM((3, 8, LOCAL), jnp.float32),
             pltpu.SemaphoreType.DMA((ROUNDS,)),
             pltpu.SemaphoreType.DMA((ROUNDS, 4)),

time: 70.9 us -> 69.6 us (0.982)
  Pallas kernels: 69.4 us -> 68.1 us
    pallas_call x1, Pallas kernels: 69.4 us -> 68.1 us  [body(): pl.pallas_call(kernel, out_shape=jax.ShapeDtypeStruct((rhs, 3, PAN), jnp....]
where the time goes in v4:
time: 69.6 us; the launch traced here: 69.4 us
  Pallas kernels  68.1 us (98%)
  local copies, waits for them, and re-layouts  1.31 us (2%)
    pallas_call x1, Pallas kernels, body(): pl.pallas_call(kernel, out_shape=jax.ShapeDtypeStruct((rhs, 3, PAN), jnp....  68.1 us

profile of v4, /device:TPU:1, one launch (start us, length us, event | category | flops | bytes accessed | tf_op | source)
XLA Modules:
  0.0 69.4 jit_solution(5824886658948313188)
XLA Ops:
  0.0 68.1 %shard_map.64 = f32[6,3,64]{2,1,0:T(4,128)} custom-call(f32[6,3,64]{2,1,0:T(4,128)} %vel_hbm.1, f32[3,64]{1,0:T(4,128)} %points_hbm.1, f32[1,64]{1,0:T(1,128)} %bitcast.6, f32[1,64]{1,0:T(1,128)} %bitcast.7, s32[16,512]{1,0:T(8,128)} %bitcast.4, f32[16,512]{1,0:T(8,128)} %bitcast.5), custom_call_target="tpu_custom_call" | custom-call | tf_op jit(solution)/shard_map/pallas_call | solution.py:491
  68.1 1.3 %copy.8 = f32[6,3,64]{2,1,0:T(4,128)} copy(f32[6,3,64]{2,1,0:T(4,128)} %shard_map.64) | data formatting | bytes 9216
